TPU v7x, 256 devices: a whole 4x4x8 slice. The times are simulated.
256 devices in a mesh: row: 8 (over x, y_hi), col: 32 (over y_lo, z, core).
Axes of the slice: x: 4, y: 4 (y_hi: 2, y_lo: 2; y = y_hi * 2 + y_lo), z: 8, core: 2. Of those that a mesh axis runs over, the one named last changes fastest.
Arguments:
- ba_left: bfloat16 [32, 2048, 128], P('col', 'row'), may hold values from -6 to 6
- ba_right: bfloat16 [32, 2048, 128], P('col', 'row'), may hold values from -0.046875 to 0.046875
- l_inverse: bfloat16 [2048, 2048], P('row', 'col'), may hold values from -1 to 1, as said below
- aa_left: bfloat16 [32, 32, 2048, 128], P('row', 'col'), may hold values from -6 to 6
- aa_right: bfloat16 [32, 32, 2048, 128], P('row', 'col'), may hold values from -0.5 to 0.5
- sketch: bfloat16 [2048, 128], replicated, may hold values from -6 to 6
- cross_tile_ranks: int32 [32], P('col'), may hold values from 32 to 128
- aa_rank: int32 [32, 32], P('row', 'col'), may hold values from 96 to 128
- target_rank: int32 [32, 32], P('row', 'col'), may hold values from 16 to 64
Outputs:
- new_left: bfloat16 [32, 32, 2048, 128], P('row', 'col')
- new_right: bfloat16 [32, 32, 2048, 128], P('row', 'col')
Inputs may be any that keep to these rules, and one draw needn't show every extreme that they name: l_inverse is lower triangular with unit diagonal.
All inputs are finite; a program needn't handle non-finite values.
Results may differ from a plain program's by a relative error of at most 0.0061.
Values may be sent and summed in bfloat16 or wider, within the bound.
No kernel may reach another device: no remote copies, remote signals or barrier semaphores. Data moves between devices by JAX's collectives and lax.ppermute only.
A program may use at most 64 MiB of HBM per device.

v0:
```python
import jax
import jax.numpy as jnp
from jax import lax
from jax.sharding import PartitionSpec as P


def in_one_piece(arrays, axis, dim, along):
    ends, at = ([], 0)
    for a in arrays[:-1]:
        at += a.shape[along]
        ends.append(at)
    both = jnp.concatenate(arrays, axis=along)
    return tuple(jnp.split(lax.all_gather(both, axis, axis=dim, tiled=True), ends, axis=along))


def joined_along(pieces, dim):
    shape = list(pieces.shape[1:])
    shape[dim] *= pieces.shape[0]
    return jnp.moveaxis(pieces, 0, dim).reshape(shape)


def copy_for_each(value, axis):
    devices = lax.axis_size(axis)
    return lax.all_to_all(
        jnp.broadcast_to(value[None], (devices, *value.shape)), axis, 0, 0, tiled=True
    )


def collect(value, axis, dim):
    return joined_along(copy_for_each(value, axis), dim)


def filled_up(lines, devices):
    spare = -lines.shape[0] % devices
    if not spare:
        return lines
    return jnp.concatenate([lines, jnp.zeros((spare, *lines.shape[1:]), lines.dtype)])


def sum_by_parts(value, axis):
    lines = value.reshape(-1, *value.shape[1:][-1:])
    own = lax.psum_scatter(
        filled_up(lines, lax.axis_size(axis)), axis, scatter_dimension=0, tiled=True
    )
    whole = lax.all_gather(own, axis).reshape(-1, *lines.shape[1:])
    return lax.slice_in_dim(whole, 0, len(lines)).reshape(value.shape)


def refresh(
    tile_left, tile_right, left_rank, goal_rank, tile_core_matrix, y_rowtile, y_coltile, sketch
):
    width = tile_left.shape[0]
    columns = jnp.arange(tile_left.shape[1], dtype=jnp.int32)
    kept_left = tile_left * (columns < left_rank).astype(jnp.bfloat16)
    probes = sketch * (columns < goal_rank).astype(jnp.bfloat16)
    sketch_core = jnp.dot(tile_right.T, probes, preferred_element_type=jnp.float32).astype(
        jnp.bfloat16
    )
    right_probe = jnp.dot(y_coltile.T, probes, preferred_element_type=jnp.float32)
    turned = jnp.dot(tile_core_matrix, right_probe, precision=lax.Precision.HIGHEST).astype(
        jnp.bfloat16
    )
    sampled = jnp.dot(kept_left, sketch_core, preferred_element_type=jnp.float32) - jnp.dot(
        y_rowtile, turned, preferred_element_type=jnp.float32
    )
    gram_matrix = jnp.dot(sampled.T, sampled, precision=lax.Precision.HIGHEST) / width
    gram_matrix = gram_matrix + jnp.diag((columns >= goal_rank).astype(jnp.float32))
    lower_cholesky_factor = jnp.linalg.cholesky(gram_matrix)
    inverse_factor = jax.scipy.linalg.solve_triangular(
        lower_cholesky_factor, jnp.eye(columns.shape[0], dtype=jnp.float32), lower=True
    )
    new_left = jnp.dot(sampled, inverse_factor.T, precision=lax.Precision.HIGHEST).astype(
        jnp.bfloat16
    )
    back_core = jnp.dot(kept_left.T, new_left, preferred_element_type=jnp.float32).astype(
        jnp.bfloat16
    )
    inner_core = jnp.dot(y_rowtile.T, new_left, preferred_element_type=jnp.float32)
    bent = jnp.dot(tile_core_matrix.T, inner_core, precision=lax.Precision.HIGHEST).astype(
        jnp.bfloat16
    )
    new_right = (
        jnp.dot(tile_right, back_core, preferred_element_type=jnp.float32)
        - jnp.dot(y_coltile, bent, preferred_element_type=jnp.float32)
    ) / width
    return (new_left, new_right.astype(jnp.bfloat16))


def select_tiles(stacked_local, row_place, col_place, row_count, col_count):
    tile_number = row_place * row_count + jnp.arange(row_count, dtype=jnp.int32)
    holder = tile_number // col_count
    local_slot = tile_number % col_count
    slots = jnp.arange(col_count, dtype=jnp.int32)
    picker = ((holder[:, None] == col_place) & (local_slot[:, None] == slots[None, :])).astype(
        jnp.bfloat16
    )
    return jnp.einsum("lk,k...->l...", picker, stacked_local, preferred_element_type=jnp.float32)


def per_device(
    ba_left, ba_right, l_inverse, aa_left, aa_right, sketch, cross_tile_ranks, aa_rank, target_rank
):
    columns = jnp.arange(ba_left.shape[-1], dtype=jnp.int32)
    u_kept = ba_left * (columns[None, None, :] < cross_tile_ranks[:, None, None]).astype(
        jnp.bfloat16
    )
    u_whole, y_whole = in_one_piece((u_kept, ba_right), "row", 1, 0)
    row_count = aa_left.shape[0]
    col_count = aa_left.shape[1]
    solved_part = jnp.einsum(
        "aw,jwr->jar", collect(l_inverse, "col", 1), u_whole, preferred_element_type=jnp.float32
    ).astype(jnp.bfloat16)
    row_place = lax.axis_index("row")
    col_place = lax.axis_index("col")
    whitened_full = collect(solved_part, "row", 1)
    stacked_whole = jnp.stack((whitened_full, y_whole), axis=1)
    picked = select_tiles(stacked_whole, row_place, col_place, row_count, col_count)
    pairs = (
        sum_by_parts(picked.astype(jnp.bfloat16), "col").astype(jnp.float32).astype(jnp.bfloat16)
    )
    whitened_rows = pairs[:, 0]
    y_rows = pairs[:, 1]
    tile_core_stack = jnp.einsum(
        "lyq,gyd->lgqd", whitened_rows, whitened_full, preferred_element_type=jnp.float32
    )
    refresh_cols = jax.vmap(refresh, in_axes=(0, 0, 0, 0, 0, None, 0, None))
    refresh_all = jax.vmap(refresh_cols, in_axes=(0, 0, 0, 0, 0, 0, None, None))
    return refresh_all(
        aa_left, aa_right, aa_rank, target_rank, tile_core_stack, y_rows, y_whole, sketch
    )


def solution(mesh):
    in_specs = (
        P("col", "row", None),
        P("col", "row", None),
        P("row", "col"),
        P("row", "col", None, None),
        P("row", "col", None, None),
        P(),
        P("col"),
        P("row", "col"),
        P("row", "col"),
    )
    out_specs = (P("row", "col", None, None), P("row", "col", None, None))
    return jax.shard_map(
        per_device, mesh=mesh, in_specs=in_specs, out_specs=out_specs, check_vma=False
    )
```

profile of v0, /device:TPU:1, one launch (start us, length us, event | category | flops | bytes accessed | tf_op | source)
XLA Modules:
  0.0 418.3 jit_solution(5768641571885218652)
XLA Ops:
  7.2 2.0 broadcast_in_dim.67
  9.2 11.1 %all-to-all-start = ((bf16[32,256,64]{1,2,0:T(8,128)(2,1)}), bf16[32,256,64]{1,2,0:T(8,128)(2,1)S(1)}, u32[]{:S(2)}, u32[]{:S(2)}) async-start(bf16[32,256,64]{1,2,0:T(8,128)(2,1)} %broadcast_in_dim.67), calls=%async_computation | async-start | bytes 2097152 | tf_op jit(solution)/shard_map/all_to_all | solution.py:24
  22.1 54.1 %all-gather.4.cloned.1.call-done = bf16[2,2048,128]{1,2,0:T(8,128)(2,1)} async-done(((bf16[2,256,128]{1,2,0:T(8,128)(2,1)}), bf16[2,2048,128]{1,2,0:T(8,128)(2,1)}) %all-gather.4.cloned.1.call-update) | async-done | bytes 1048592 | tf_op jit(solution)/shard_map/all_gather | solution.py:13
  76.2 1.3 fusion.29
  77.6 0.8 broadcast_in_dim.69
  78.4 3.5 all-to-all-start.1
  82.0 1.9 slice_bitcast_fusion.7
  83.9 6.6 %all-to-all-done.1 = bf16[8,1,256,128]{2,3,1,0:T(8,128)(2,1)S(1)} async-done(((bf16[8,1,256,128]{2,3,1,0:T(8,128)(2,1)}), bf16[8,1,256,128]{2,3,1,0:T(8,128)(2,1)S(1)}, u32[]{:S(2)}, u32[]{:S(2)}) %all-to-all-start.1) | async-done | bytes 524320 | tf_op jit(solution)/shard_map/all_to_all | solution.py:24
  91.0 2.5 fusion.30
  93.5 2.9 copy.61
  96.4 4.3 %multiply_convert_fusion = bf16[4,2,2048,128]{3,2,1,0:T(8,128)(2,1)} fusion(f32[2,2048,128]{2,1,0:T(8,128)} %copy.61, f32[4]{0:T(128)S(1)} %compare_convert_fusion.1), kind=kLoop, calls=%fused_computation | loop fusion | flops 4194304 | bytes 6291472 | tf_op jit(solution)/shard_map/convert_element_type | solution.py:119
  100.9 121.7 %reduce-scatter.2.cloned.1.call-done = bf16[512,128]{1,0:T(8,128)(2,1)} async-done(((bf16[16384,128]{1,0:T(8,128)(2,1)}), bf16[512,128]{1,0:T(8,128)(2,1)}) %reduce-scatter.2.cloned.1.call-update) | async-done | bytes 131088 | tf_op jit(solution)/shard_map/reduce_scatter | solution.py:42
  223.0 5.0 %fusion.11 = f32[4,2048,128]{2,1,0:T(8,128)} fusion(bf16[4,1,2048,128]{3,2,1,0:T(8,128)(2,1)} %param.12, bf16[4,1,2048,128]{3,2,1,0:T(8,128)(2,1)S(1)} %copy-done, bf16[4,128]{1,0:T(4,128)(2,1)S(1)} %get-tuple-element.11, bf16[2048,128]{1,0:T(8,128)(2,1)S(1)} %copy-done.5, bf16[4,128]{1,0:T(4,128)(2,1)S(1)} %get-tuple-element.12), kind=kOutput, calls=%fused_computation.17 | convolution fusion | flops 539033600 | bytes 8914944 | tf_op jit(solution)/shard_map/vmap(vmap())/dot_general | solution.py:63
  228.0 2.2 fusion.2
  230.4 60.3 %all-gather.6.cloned.1.call-done = bf16[16384,128]{1,0:T(8,128)(2,1)} async-done(((bf16[512,128]{1,0:T(8,128)(2,1)}), bf16[16384,128]{1,0:T(8,128)(2,1)}) %all-gather.6.cloned.1.call-update) | async-done | bytes 4194320 | tf_op jit(solution)/shard_map/all_gather | solution.py:45
  290.7 2.0 fusion.6
  293.4 3.5 convolution_subtract_fusion
  296.9 7.0 %fusion.16 = f32[4,128,128]{1,2,0:T(8,128)S(1)} fusion(f32[4,2048,128]{2,1,0:T(8,128)S(1)} %convolution_subtract_fusion, f32[4,128]{1,0:T(4,128)S(1)} %get-tuple-element.10, pred[128,128]{0,1:T(8,128)(4,1)S(1)} %copy.68), kind=kOutput, calls=%fused_computation.23 | convolution fusion | flops 1610809344 | bytes 4474880 | tf_op jit(solution)/shard_map/vmap(vmap())/dot_general | solution.py:66
  304.0 47.1 %custom-call.8 = f32[4,1,128,128]{3,2,1,0:T(8,128)S(1)} custom-call(f32[4,1,128,128]{3,2,1,0:T(8,128)S(1)} %fusion.47), custom_call_target="Cholesky" | custom-call | tf_op jit(solution)/shard_map/vmap(vmap(jit(cholesky)))/cholesky | solution.py:68
  351.4 39.3 %custom-call.9 = f32[4,1,1,128,128]{3,4,2,1,0:T(8,128)S(1)} custom-call(f32[4,1,1,128,128]{4,3,2,1,0:T(8,128)S(1)} %fusion.54), custom_call_target="InvertDiagBlocksLowerTriangular" | custom-call | tf_op jit(solution)/shard_map/vmap(vmap(jit(_solve_triangular)))/triangular_solve | solution.py:69
  391.4 5.5 %convolution_convert_fusion = bf16[4,2048,128]{2,1,0:T(8,128)(2,1)S(1)} fusion(f32[4,2048,128]{2,1,0:T(8,128)} %copy-done.1, f32[4,128,128]{2,1,0:T(8,128)S(1)} %fusion.49), kind=kOutput, calls=%fused_computation.5 | convolution fusion | flops 1611661312 | bytes 6553600 | tf_op jit(solution)/shard_map/vmap(vmap())/dot_general | solution.py:72
  398.9 2.7 fusion.41
  401.6 6.2 %fusion.1 = bf16[4,1,2048,128]{2,3,0,1:T(8,128)(2,1)} fusion(f32[2048,4,128]{0,2,1:T(8,128)} %fusion.41, bf16[4,1,2048,128]{3,2,1,0:T(8,128)(2,1)S(1)} %copy-done, bf16[4,2048,128]{2,1,0:T(8,128)(2,1)} %copy-done.2, bf16[4,1,2048,128]{3,2,1,0:T(8,128)(2,1)} %param.12, bf16[4,128]{1,0:T(4,128)(2,1)S(1)} %get-tuple-element.12), kind=kOutput, calls=%fused_computation.3 | convolution fusion | flops 541130752 | bytes 12583936 | tf_op jit(solution)/shard_map/vmap(vmap())/dot_general | solution.py:83
  407.8 3.9 copy.79
  (52 shorter events, 6.0 us)
Async XLA Ops:
  7.2 215.8 %copy-start = (bf16[4,1,2048,128]{3,2,1,0:T(8,128)(2,1)S(1)}, bf16[4,1,2048,128]{3,2,1,0:T(8,128)(2,1)}, u32[]{:S(2)}) copy-start(bf16[4,1,2048,128]{3,2,1,0:T(8,128)(2,1)} %param.13) | copy-start | bytes 6291460
  7.2 13.9 %copy-start.7 = (bf16[1,256,128]{2,1,0:T(8,128)(2,1)S(1)}, bf16[1,256,128]{2,1,0:T(8,128)(2,1)}, u32[]{:S(2)}) copy-start(bf16[1,256,128]{2,1,0:T(8,128)(2,1)} %param.9) | copy-start | bytes 196612
  7.2 14.1 %copy-start.8 = (bf16[1,256,128]{2,1,0:T(8,128)(2,1)S(1)}, bf16[1,256,128]{2,1,0:T(8,128)(2,1)}, u32[]{:S(2)}) copy-start(bf16[1,256,128]{2,1,0:T(8,128)(2,1)} %param.10) | copy-start | bytes 196612
  9.2 67.0 %all-to-all-start = ((bf16[32,256,64]{1,2,0:T(8,128)(2,1)}), bf16[32,256,64]{1,2,0:T(8,128)(2,1)S(1)}, u32[]{:S(2)}, u32[]{:S(2)}) async-start(bf16[32,256,64]{1,2,0:T(8,128)(2,1)} %broadcast_in_dim.67), calls=%async_computation | async-start | bytes 2097152 | tf_op jit(solution)/shard_map/all_to_all | solution.py:24
  20.3 55.9 %all-gather.4.cloned.1.call-start = ((), (), s32[]{:S(2)}) async-start(), calls=%async_computation.3 | async-start | bytes 1179648 | tf_op jit(solution)/shard_map/all_gather | solution.py:13
  78.4 12.0 %all-to-all-start.1 = ((bf16[8,1,256,128]{2,3,1,0:T(8,128)(2,1)}), bf16[8,1,256,128]{2,3,1,0:T(8,128)(2,1)S(1)}, u32[]{:S(2)}, u32[]{:S(2)}) async-start(bf16[8,1,256,128]{2,3,1,0:T(8,128)(2,1)} %broadcast_in_dim.69), calls=%async_computation.1 | async-start | bytes 1048576 | tf_op jit(solution)/shard_map/all_to_all | solution.py:24
  81.9 140.7 %reduce-scatter.2.cloned.1.call-start = ((), (), s32[]{:S(2)}) async-start(), calls=%async_computation.4 | async-start | bytes 4325376 | tf_op jit(solution)/shard_map/reduce_scatter | solution.py:42
  100.7 122.2 %copy-start.9 = (s32[4,1]{0,1:T(1,128)S(1)}, s32[4,1]{0,1:T(1,128)}, u32[]{:S(2)}) copy-start(s32[4,1]{0,1:T(1,128)} %param.17) | copy-start | bytes 52
  100.7 122.2 %copy-start.10 = (s32[4,1]{0,1:T(1,128)S(1)}, s32[4,1]{0,1:T(1,128)}, u32[]{:S(2)}) copy-start(s32[4,1]{0,1:T(1,128)} %param.16) | copy-start | bytes 52
  100.7 122.3 %copy-start.5 = (bf16[2048,128]{1,0:T(8,128)(2,1)S(1)}, bf16[2048,128]{1,0:T(8,128)(2,1)}, u32[]{:S(2)}) copy-start(bf16[2048,128]{1,0:T(8,128)(2,1)} %param.14) | copy-start | bytes 1572868
  100.7 190.0 %all-gather.6.cloned.1.call-start = ((), (), s32[]{:S(2)}) async-start(), calls=%async_computation.5 | async-start | bytes 4325376 | tf_op jit(solution)/shard_map/all_gather | solution.py:45
  230.4 62.3 %copy-start.6 = (f32[128,4,128]{2,0,1:T(8,128)S(1)}, f32[128,4,128]{2,0,1:T(8,128)}, u32[]{:S(2)}) copy-start(f32[128,4,128]{2,0,1:T(8,128)} %fusion.2) | copy-start | bytes 786436
  296.9 7.0 %copy-start.1 = (f32[4,2048,128]{2,1,0:T(8,128)}, f32[4,2048,128]{2,1,0:T(8,128)S(1)}, u32[]{:S(2)}) copy-start(f32[4,2048,128]{2,1,0:T(8,128)S(1)} %convolution_subtract_fusion) | copy-start | bytes 12582916
  391.4 5.5 %copy-start.4 = (bf16[16384,128]{1,0:T(8,128)(2,1)S(1)}, bf16[16384,128]{1,0:T(8,128)(2,1)}, u32[]{:S(2)}) copy-start(bf16[16384,128]{1,0:T(8,128)(2,1)} %all-gather.6.cloned.1.call-done) | copy-start | bytes 12582916
  396.9 1.3 copy-start.2
  396.9 2.0 copy-start.3
Sparse Core Ops, SparseCore 0:
  24.2 51.9 all-gather.3
  100.8 121.7 reduce-scatter.1
  224.5 66.1 all-gather.5
where the time goes:
time: 419 us; the launch traced here: 418 us
  waiting for transfers between devices  243 us (58%)
  other arithmetic  94.4 us (23%)
  matrix products  37.8 us (9%)
  starting transfers between devices  14.9 us (4%)
  between operations  14.7 us (4%)
  local copies, waits for them, and re-layouts  13.6 us (3%)
    reduce_scatter x1, waiting for transfers between devices, sum_by_parts(): lax.psum_scatter(filled_up(lines, lax.axis_size(axis)), axis, scatter_dim...  122 us
    all_gather x1, waiting for transfers between devices, sum_by_parts(): whole = lax.all_gather(own, axis).reshape(-1, *lines.shape[1:])  60.3 us
    all_gather x1, waiting for transfers between devices, in_one_piece(): lax.all_gather(both, axis, axis=dim, tiled=True)  54.1 us
    another operation x4, other arithmetic, refresh(): lower_cholesky_factor = jnp.linalg.cholesky(gram_matrix)  47.3 us
    another operation x3, other arithmetic, refresh(): jax.scipy.linalg.solve_triangular(lower_cholesky_factor, jnp.eye(columns....  39.4 us
    all_to_all x2, starting transfers between devices, copy_for_each(): lax.all_to_all(jnp.broadcast_to(value[None], (devices, *value.shape)), ax...  14.6 us
  transfers between devices with their start and end apart: 5, of which 4 were waited for; matrix products, arithmetic and copies ran while one was open for 3% of the time, Pallas kernels for 0%

commit v1 on v0

v1 whole, which is shorter than its diff:
```python
import jax
import jax.numpy as jnp
from jax import lax
from jax.experimental import pallas as pl
from jax.experimental.pallas import tpu as pltpu
from jax.sharding import Mesh
from jax.sharding import PartitionSpec as P

BF = jnp.bfloat16
F32 = jnp.float32
HI = lax.Precision.HIGHEST
TILE = 2048
RANK = 128
GOAL = 64
ROWS = 8
COLS = 32
OWN = 4
ROW = ("x", "yh")
COL = ("yl", "z", "core")
ALL = ("x", "yh", "yl", "z", "core")
SWAP = [(0, 1), (1, 0)]


def to_tile_rows():
    return [
        (r * COLS + c, (c // OWN) * COLS + (c % OWN) * ROWS + r)
        for r in range(ROWS)
        for c in range(COLS)
    ]


def gathered(value, axis, count):
    return lax.all_to_all(
        jnp.broadcast_to(value[None], (count, *value.shape)), axis, 0, 0, tiled=True
    )


def dot_tn(a, b, precision=None):
    return lax.dot_general(
        a, b, (((0,), (0,)), ((), ())), precision=precision, preferred_element_type=F32
    )


def dot_nt(a, b, precision=None):
    return lax.dot_general(
        a, b, (((1,), (1,)), ((), ())), precision=precision, preferred_element_type=F32
    )


def dot_nn(a, b, precision=None):
    return lax.dot_general(
        a, b, (((1,), (0,)), ((), ())), precision=precision, preferred_element_type=F32
    )


def solve_kernel(lt_ref, u_ref, out_ref):
    solved_t = dot_tn(u_ref[...], lt_ref[...]).astype(BF)
    out_ref[...] = dot_nt(lt_ref[...], solved_t).astype(BF)


def solve(l_rows_t, u_whole):
    return pl.pallas_call(
        solve_kernel,
        out_shape=jax.ShapeDtypeStruct((TILE, RANK), BF),
        cost_estimate=pl.CostEstimate(
            flops=4 * TILE * 256 * RANK, bytes_accessed=2 << 20, transcendentals=0
        ),
        name="solve",
    )(l_rows_t, u_whole)


def before_kernel(
    rank_ref, goal_ref, left_ref, right_ref, y_ref, u_ref, sketch_ref,
    gram_ref, probe_ref, turn_ref,
):
    k = pl.program_id(0)
    both = jnp.concatenate([left_ref[0], y_ref[0]], axis=1)
    gram = dot_tn(both, both)
    first = gram.astype(BF)
    rest = gram - first.astype(F32)
    second = rest.astype(BF)
    third = (rest - second.astype(F32)).astype(BF)
    gram_ref[0, 0:256, :] = first
    gram_ref[0, 256:512, :] = second
    gram_ref[0, 512:768, :] = third
    core = dot_tn(right_ref[0], sketch_ref[...])
    row = lax.broadcasted_iota(jnp.int32, (RANK, RANK), 0)
    col = lax.broadcasted_iota(jnp.int32, (RANK, RANK), 1)
    keep = (row < rank_ref[k]) & (col < goal_ref[k])
    probe_ref[0] = jnp.where(keep, core, 0.0).astype(BF)
    turn_ref[0] = u_ref[0].T


def before(ranks, goals, left, right, y_rows, u_rows, sketch):
    tile = pl.BlockSpec((1, TILE, RANK), lambda k, *_: (k, 0, 0))
    return pl.pallas_call(
        before_kernel,
        grid_spec=pltpu.PrefetchScalarGridSpec(
            num_scalar_prefetch=2,
            grid=(OWN,),
            in_specs=[tile, tile, tile, tile, pl.BlockSpec((TILE, RANK), lambda k, *_: (0, 0))],
            out_specs=[
                pl.BlockSpec((1, 768, 256), lambda k, *_: (k, 0, 0)),
                pl.BlockSpec((1, RANK, RANK), lambda k, *_: (k, 0, 0)),
                pl.BlockSpec((1, RANK, TILE), lambda k, *_: (k, 0, 0)),
            ],
        ),
        out_shape=[
            jax.ShapeDtypeStruct((OWN, 768, 256), BF),
            jax.ShapeDtypeStruct((OWN, RANK, RANK), BF),
            jax.ShapeDtypeStruct((OWN, RANK, TILE), BF),
        ],
        cost_estimate=pl.CostEstimate(
            flops=OWN * 2 * TILE * (256 * 256 + RANK * RANK),
            bytes_accessed=12 << 20,
            transcendentals=0,
        ),
        name="before",
    )(ranks, goals, left, right, y_rows, u_rows, sketch)


def whitening(grams):
    lane = lax.broadcasted_iota(jnp.int32, (8, RANK), 1)
    sub = lax.broadcasted_iota(jnp.int32, (8, RANK), 0)
    blocks = []
    for gram in grams:
        own = []
        for b in range(8):
            unit = jnp.where(lane == sub + (8 * b + GOAL), 1.0, 0.0)
            own.append(jnp.where(lane < GOAL, gram[8 * b : 8 * b + 8, :], unit))
        blocks.append(own)
    for k in range(GOAL - 1):
        kb, ks = k // 8, k % 8
        for own in blocks:
            pivot_row = jnp.broadcast_to(own[kb][ks : ks + 1, :], (8, RANK))
            pivot = jnp.broadcast_to(own[kb][ks : ks + 1, k : k + 1], (8, RANK))
            scaled = pivot_row / pivot
            for b in range(kb, 8):
                if b == kb and ks == 7:
                    continue
                column = jnp.broadcast_to(own[b][:, k : k + 1], (8, RANK))
                if b == kb:
                    column = jnp.where(sub > ks, column, 0.0)
                own[b] = own[b] - column * scaled
    factors = []
    for own in blocks:
        done = []
        for b in range(8):
            diagonal = jnp.sum(
                jnp.where(lane == sub + 8 * b, own[b], 0.0), axis=1, keepdims=True
            )
            scale = 1.0 / jnp.sqrt(diagonal)
            moved = pltpu.roll(own[b], GOAL, 1)
            done.append(jnp.where(lane < GOAL, moved * scale, 0.0))
        factors.append(jnp.concatenate(done, axis=0))
    return factors


def after_kernel(
    rank_ref, goal_ref, gram_ref, probe_ref, turn_ref, v_ref, yc_ref, sketch_ref,
    left_hbm, right_hbm, y_hbm,
    out_left, out_right,
    left, right, y_rows, new_left, new_right, in_sem, out_sem,
):
    loads = []
    for n, (source, target) in enumerate(((left_hbm, left), (y_hbm, y_rows), (right_hbm, right))):
        copy = pltpu.make_async_copy(source, target, in_sem.at[n])
        copy.start()
        loads.append(copy)
    row = lax.broadcasted_iota(jnp.int32, (RANK, RANK), 0)
    col = lax.broadcasted_iota(jnp.int32, (RANK, RANK), 1)
    right_probe = dot_tn(yc_ref[...], sketch_ref[...])
    cores, probes, pushed, grams = [], [], [], []
    for k in range(OWN):
        core = dot_nn(turn_ref[k], v_ref[...])
        turned = dot_nn(core, jnp.where(col < goal_ref[k], right_probe, 0.0), HI)
        probe = jnp.concatenate([probe_ref[k], (-turned).astype(BF)], axis=0)
        three = dot_nn(gram_ref[k], probe)
        push = three[0:256] + (three[256:512] + three[512:768])
        gram = dot_tn(probe.astype(F32), push, HI) * (1.0 / TILE)
        gram = gram + jnp.where((row == col) & (col >= goal_ref[k]), 1.0, 0.0)
        cores.append(core)
        probes.append(probe)
        pushed.append(push)
        grams.append(gram[0:GOAL, :])
    factors = whitening(grams)
    zeros = jnp.zeros((RANK - GOAL, RANK), F32)
    for copy in loads:
        copy.wait()
    stores = []
    for k in range(OWN):
        factor = jnp.concatenate([factors[k], zeros], axis=0)
        mixed = dot_nt(probes[k].astype(F32), factor, HI)
        high = mixed.astype(BF)
        low = (mixed - high.astype(F32)).astype(BF)
        both = jnp.concatenate([left[k], y_rows[k]], axis=1)
        new_left[k] = (dot_nn(both, high) + dot_nn(both, low)).astype(BF)
        copy = pltpu.make_async_copy(new_left.at[k], out_left.at[k], out_sem.at[0, k])
        copy.start()
        stores.append(copy)
        seen = dot_nt(pushed[k], factor, HI)
        back = jnp.where(row < rank_ref[k], seen[0:RANK], 0.0).astype(BF)
        bent = dot_tn(cores[k], seen[RANK:], HI).astype(BF)
        pair = jnp.concatenate([right[k], yc_ref[...]], axis=1)
        answer = dot_nn(pair, jnp.concatenate([back, -bent], axis=0))
        new_right[k] = (answer * (1.0 / TILE)).astype(BF)
        copy = pltpu.make_async_copy(new_right.at[k], out_right.at[k], out_sem.at[1, k])
        copy.start()
        stores.append(copy)
    for copy in stores:
        copy.wait()


def after(ranks, goals, gram, probe, turn, v_whole, y_whole, sketch, left, right, y_rows):
    smem = pl.BlockSpec(memory_space=pltpu.SMEM)
    vmem = pl.BlockSpec(memory_space=pltpu.VMEM)
    hbm = pl.BlockSpec(memory_space=pl.ANY)
    whole = jax.ShapeDtypeStruct((OWN, TILE, RANK), BF)
    return pl.pallas_call(
        after_kernel,
        in_specs=[smem, smem] + [vmem] * 6 + [hbm] * 3,
        out_specs=[hbm, hbm],
        out_shape=[whole, whole],
        scratch_shapes=[pltpu.VMEM((OWN, TILE, RANK), BF)] * 5
        + [pltpu.SemaphoreType.DMA((3,)), pltpu.SemaphoreType.DMA((2, OWN))],
        cost_estimate=pl.CostEstimate(
            flops=OWN * 2 * TILE * 256 * RANK * 4, bytes_accessed=16 << 20, transcendentals=0
        ),
        name="after",
    )(ranks, goals, gram, probe, turn, v_whole, y_whole, sketch, left, right, y_rows)


def per_device(
    ba_left, ba_right, l_inverse, aa_left, aa_right, sketch, cross_tile_ranks, aa_rank, target_rank
):
    columns = jnp.arange(RANK, dtype=jnp.int32)
    u_kept = jnp.where(columns[None, :] < cross_tile_ranks[0], ba_left[0], jnp.zeros((), BF))
    ranks, goals = aa_rank[:, 0], target_rank[:, 0]
    left, right = aa_left[:, 0], aa_right[:, 0]
    own = jnp.stack([u_kept, ba_right[0]])
    bulk = lax.all_gather(lax.ppermute(own, ALL, to_tile_rows()), COL, axis=1)
    bulk = bulk.reshape(2, OWN, TILE, RANK)
    u_rows, y_rows = bulk[0], bulk[1]
    l_own = l_inverse.T
    l_pair = lax.ppermute(l_own, "yl", SWAP)
    here = lax.axis_index("yl") == 0
    l_pair = jnp.stack([jnp.where(here, l_own, l_pair), jnp.where(here, l_pair, l_own)])
    l_half = gathered(l_pair, "z", 8)
    l_other = lax.ppermute(l_half, "core", SWAP)
    first = lax.axis_index("core") == 0
    l_rows_t = jnp.stack(
        [jnp.where(first, l_half, l_other), jnp.where(first, l_other, l_half)], axis=2
    )
    l_rows_t = l_rows_t.swapaxes(0, 1).reshape(TILE, 256)
    u_whole = gathered(u_kept, ROW, ROWS).reshape(TILE, RANK)
    y_whole = gathered(ba_right[0], ROW, ROWS).reshape(TILE, RANK)
    v_part = solve(l_rows_t, u_whole)
    v_parts = lax.all_to_all(v_part.reshape(ROWS, 256, RANK), ROW, 0, 0, tiled=True)
    v_own = jnp.sum(v_parts.astype(F32), axis=0).astype(BF)
    v_whole = gathered(v_own, ROW, ROWS).reshape(TILE, RANK)
    gram, probe, turn = before(ranks, goals, left, right, y_rows, u_rows, sketch)
    new_left, new_right = after(
        ranks, goals, gram, probe, turn, v_whole, y_whole, sketch, left, right, y_rows
    )
    return new_left[:, None], new_right[:, None]


def solution(mesh):
    fine = Mesh(mesh.devices.reshape(4, 2, 2, 8, 2), ALL)
    in_specs = (
        P(COL, ROW, None),
        P(COL, ROW, None),
        P(ROW, COL),
        P(ROW, COL, None, None),
        P(ROW, COL, None, None),
        P(),
        P(COL),
        P(ROW, COL),
        P(ROW, COL),
    )
    out_specs = (P(ROW, COL, None, None), P(ROW, COL, None, None))
    return jax.shard_map(
        per_device, mesh=fine, in_specs=in_specs, out_specs=out_specs, check_vma=False
    )
```

time: 419 us -> 163 us (0.39)
  waiting for transfers between devices: 243 us -> 22.8 us
  other arithmetic: 94.4 us -> 2.74 us
  blocking collectives: 0 us -> 45.9 us
  matrix products: 37.8 us -> 0 us
  Pallas kernels: 0 us -> 35.3 us
  starting transfers between devices: 14.9 us -> 29.4 us
    reduce_scatter x1 -> x0, waiting for transfers between devices: 122 us -> none  [sum_by_parts(): lax.psum_scatter(filled_up(lines, lax.axis_size(axis)), axis, scatter_dim...]
    all_gather x2 -> x1, waiting for transfers between devices: 114 us -> 0.01 us  [per_device(): bulk = lax.all_gather(lax.ppermute(own, ALL, to_tile_rows()), COL, axis=1)]
    another operation x9 -> x4, other arithmetic: 89.2 us -> 1.7 us  [the longest x1 0.85 us: per_device(): own = jnp.stack([u_kept, ba_right[0]])]
    all_to_all x0 -> x2, blocking collectives: none -> 45.9 us  [the longest x1 31.1 us: gathered(): lax.all_to_all(jnp.broadcast_to(value[None], (count, *value.shape)), axis...]
    dot_general x12 -> x0, matrix products: 37.2 us -> none  [the longest x1 6.95 us: refresh(): jnp.dot(sampled.T, sampled, precision=lax.Precision.HIGHEST) / width]
    pallas_call x0 -> x3, Pallas kernels: none -> 35.3 us  [the longest x1 24.3 us: after(): pl.pallas_call(after_kernel, in_specs=[smem, smem] + [vmem] * 6 + [hbm] *...]
    ppermute x0 -> x3, starting transfers between devices: none -> 13.9 us  [the longest x1 10.2 us: per_device(): bulk = lax.all_gather(lax.ppermute(own, ALL, to_tile_rows()), COL, axis=1)]
    all_to_all x2 -> x3, waiting for transfers between devices: 6.61 us -> 19.3 us  [gathered(): lax.all_to_all(jnp.broadcast_to(value[None], (count, *value.shape)), axis...]
  transfers between devices with their start and end apart: 5 -> 7, of which waited for: 4 -> 4; matrix products, arithmetic and copies ran while one was open for 3% -> 6% of each run, Pallas kernels for 0% -> 7%
where the time goes in v1:
time: 163 us; the launch traced here: 161 us
  blocking collectives  45.9 us (28%)
  Pallas kernels  35.3 us (22%)
  starting transfers between devices  29.4 us (18%)
  waiting for transfers between devices  22.8 us (14%)
  between operations  14.8 us (9%)
  local copies, waits for them, and re-layouts  10.5 us (6%)
  other arithmetic  2.74 us (2%)
    all_to_all x1, blocking collectives, gathered(): lax.all_to_all(jnp.broadcast_to(value[None], (count, *value.shape)), axis...  31.1 us
    pallas_call x1, Pallas kernels, after(): pl.pallas_call(after_kernel, in_specs=[smem, smem] + [vmem] * 6 + [hbm] *...  24.3 us
    all_to_all x3, waiting for transfers between devices, gathered(): lax.all_to_all(jnp.broadcast_to(value[None], (count, *value.shape)), axis...  19.3 us
    all_to_all x3, starting transfers between devices, gathered(): lax.all_to_all(jnp.broadcast_to(value[None], (count, *value.shape)), axis...  15.4 us
    all_to_all x1, blocking collectives, per_device(): lax.all_to_all(v_part.reshape(ROWS, 256, RANK), ROW, 0, 0, tiled=True)  14.8 us
    ppermute x1, starting transfers between devices, per_device(): bulk = lax.all_gather(lax.ppermute(own, ALL, to_tile_rows()), COL, axis=1)  10.2 us
    pallas_call x1, Pallas kernels, before(): pl.pallas_call(before_kernel, grid_spec=pltpu.PrefetchScalarGridSpec(num_...  7.8 us
    slice x1, local copies, waits for them, and re-layouts, per_device(): u_rows, y_rows = (bulk[0], bulk[1])  4.54 us
  transfers between devices with their start and end apart: 7, of which 4 were waited for; matrix products, arithmetic and copies ran while one was open for 6% of the time, Pallas kernels for 7%

profile of v1, /device:TPU:1, one launch (start us, length us, event | category | flops | bytes accessed | tf_op | source)
XLA Modules:
  0.0 161.5 jit_solution(4343045337339717245)
XLA Ops:
  7.9 0.9 broadcast_select_fusion
  8.7 0.9 pad_maximum_fusion
  9.6 10.2 %collective-permute-start = (bf16[2,256,128]{2,1,0:T(8,128)(2,1)S(1)}, bf16[2,256,128]{2,1,0:T(8,128)(2,1)S(1)}, u32[]{:S(2)}, u32[]{:S(2)}) collective-permute-start(bf16[2,256,128]{2,1,0:T(8,128)(2,1)S(1)} %pad_maximum_fusion), channel_id=1, source_target_pairs={{0,0},{1,8},{2,16},{3,24},{4,32},{5,40},{6,48},{7,56},{8,64},{9,72... | collective-permute-start | bytes 393224 | tf_op jit(solution)/shard_map/ppermute | solution.py:241
  19.8 1.9 %collective-permute-done = bf16[2,256,128]{2,1,0:T(8,128)(2,1)S(1)} collective-permute-done((bf16[2,256,128]{2,1,0:T(8,128)(2,1)S(1)}, bf16[2,256,128]{2,1,0:T(8,128)(2,1)S(1)}, u32[]{:S(2)}, u32[]{:S(2)}) %collective-permute-start) | collective-permute-done | bytes 131104 | tf_op jit(solution)/shard_map/ppermute | solution.py:241
  22.4 3.7 %collective-permute-start.1 = (bf16[64,256]{1,0:T(8,128)(2,1)}, bf16[64,256]{1,0:T(8,128)(2,1)S(1)}, u32[]{:S(2)}, u32[]{:S(2)}) collective-permute-start(bf16[64,256]{1,0:T(8,128)(2,1)} %bitcast.48), channel_id=1, source_target_pairs={{0,16},{16,0},{1,17},{17,1},{2,18},{18,2},{3,19},{19,3},{4,20},{20... | collective-permute-start | bytes 98312 | tf_op jit(solution)/shard_map/ppermute | solution.py:245
  26.2 1.5 collective-permute-done.1
  27.7 0.8 select_bitcast_fusion.3
  28.5 31.1 %all_to_all.25 = bf16[8,2,64,256]{3,2,1,0:T(8,128)(2,1)S(1)} all-to-all(bf16[8,2,64,256]{3,2,1,0:T(8,128)(2,1)S(1)} %broadcast_in_dim.48), channel_id=1, replica_groups=mesh['x'=4,'yh'=2,'yl'=2,'z'=8,'core'=2] {'z'}, dimensions={0} | all-to-all | bytes 1048576 | tf_op jit(solution)/shard_map/all_to_all | solution.py:33
  59.6 0.9 broadcast_in_dim.50
  60.5 6.4 %all-to-all-start.1 = ((bf16[8,256,128]{2,1,0:T(8,128)(2,1)}), bf16[8,256,128]{2,1,0:T(8,128)(2,1)S(1)}, u32[]{:S(2)}, u32[]{:S(2)}) async-start(bf16[8,256,128]{2,1,0:T(8,128)(2,1)} %broadcast_in_dim.50), calls=%async_computation.1 | async-start | bytes 1048576 | tf_op jit(solution)/shard_map/all_to_all | solution.py:33
  67.0 1.0 copy.14
  68.1 9.2 %all-to-all-done.1 = bf16[8,256,128]{2,1,0:T(8,128)(2,1)S(1)} async-done(((bf16[8,256,128]{2,1,0:T(8,128)(2,1)}), bf16[8,256,128]{2,1,0:T(8,128)(2,1)S(1)}, u32[]{:S(2)}, u32[]{:S(2)}) %all-to-all-start.1) | async-done | bytes 524320 | tf_op jit(solution)/shard_map/all_to_all | solution.py:33
  77.3 0.8 copy-done.2
  78.1 3.2 %solve.1 = bf16[2048,128]{1,0:T(8,128)(2,1)} custom-call(bf16[2048,256]{1,0:T(8,128)(2,1)} %bitcast.42, bf16[2048,128]{1,0:T(8,128)(2,1)} %bitcast.45), custom_call_target="tpu_custom_call" | custom-call | flops 268435456 | bytes 2097152 | tf_op jit(solution)/shard_map/solve/pallas_call | solution.py:62
  81.3 14.8 %all_to_all.26 = bf16[8,256,128]{2,1,0:T(8,128)(2,1)S(1)} all-to-all(bf16[8,256,128]{2,1,0:T(8,128)(2,1)} %bitcast.46), channel_id=1, replica_groups=mesh['x'=4,'yh'=2,'yl'=2,'z'=8,'core'=2] {'x','yh'}, dimensions={0} | all-to-all | bytes 1048576 | tf_op jit(solution)/shard_map/all_to_all | solution.py:258
  96.1 0.9 broadcast_in_dim.53
  96.9 5.3 %all-to-all-start.4 = ((bf16[8,256,128]{2,1,0:T(8,128)(2,1)}), bf16[8,256,128]{2,1,0:T(8,128)(2,1)S(1)}, u32[]{:S(2)}, u32[]{:S(2)}) async-start(bf16[8,256,128]{2,1,0:T(8,128)(2,1)} %broadcast_in_dim.53), calls=%async_computation.4 | async-start | bytes 1048576 | tf_op jit(solution)/shard_map/all_to_all | solution.py:33
  102.4 10.1 %all-to-all-done.4 = bf16[8,256,128]{2,1,0:T(8,128)(2,1)S(1)} async-done(((bf16[8,256,128]{2,1,0:T(8,128)(2,1)}), bf16[8,256,128]{2,1,0:T(8,128)(2,1)S(1)}, u32[]{:S(2)}, u32[]{:S(2)}) %all-to-all-start.4) | async-done | bytes 524320 | tf_op jit(solution)/shard_map/all_to_all | solution.py:33
  112.5 0.9 broadcast_in_dim.51
  113.4 3.7 %all-to-all-start.3 = ((bf16[8,256,128]{2,1,0:T(8,128)(2,1)}), bf16[8,256,128]{2,1,0:T(8,128)(2,1)S(1)}, u32[]{:S(2)}, u32[]{:S(2)}) async-start(bf16[8,256,128]{2,1,0:T(8,128)(2,1)} %broadcast_in_dim.51), calls=%async_computation.3 | async-start | bytes 1048576 | tf_op jit(solution)/shard_map/all_to_all | solution.py:33
  117.2 4.5 %fusion = (bf16[1,8192,128]{2,1,0:T(8,128)(2,1)}, bf16[1,8192,128]{2,1,0:T(8,128)(2,1)}) fusion(bf16[2,8192,128]{2,1,0:T(8,128)(2,1)} %all-gather.3.cloned.1.call-done), kind=kLoop, calls=%fused_computation.9 | loop fusion | bytes 8388608 | tf_op jit(solution)/shard_map/slice | solution.py:243
  121.7 7.8 %before.1 = (bf16[4,768,256]{2,1,0:T(8,128)(2,1)}, bf16[4,128,128]{2,1,0:T(8,128)(2,1)}, bf16[4,128,2048]{2,1,0:T(8,128)(2,1)}) custom-call(s32[4]{0:T(128)} %bitcast.49, s32[4]{0:T(128)} %bitcast.51, bf16[4,2048,128]{2,1,0:T(8,128)(2,1)} %bitcast.37, bf16[4,2048,128]{2,1,0:T(8,128)(2,1)} %bitcast.39, bf16[4,2048,128]{2,1,0:T(8,128)(2,1)} %bitcast.35, ...), custom_call_target="tpu_custom_call" | custom-call | flops 1342177280 | bytes 12582912 | tf_op jit(solution)/shard_map/before/pallas_call | solution.py:96
  129.5 0.8 copy-done.1
  130.3 24.3 %after.1 = (bf16[4,2048,128]{2,1,0:T(8,128)(2,1)}, bf16[4,2048,128]{2,1,0:T(8,128)(2,1)}) custom-call(s32[4]{0:T(128)} %bitcast.50, s32[4]{0:T(128)} %bitcast.52, bf16[4,768,256]{2,1,0:T(8,128)(2,1)} %get-tuple-element.7.gram_ref, bf16[4,128,128]{2,1,0:T(8,128)(2,1)} %get-tuple-element.8.probe_ref, bf16[4,128,2048]{2,1,0:T(8,128)(2,1)} %get-tuple-element.9.turn_ref, ...), custom_call_target="tpu_custom_call" | custom-call | flops 2147483648 | bytes 16777216 | tf_op jit(solution)/shard_map/after/pallas_call | solution.py:219
  (23 shorter events, 1.1 us)
Async XLA Ops:
  7.2 52.4 %copy-start.3 = (bf16[1,256,128]{2,1,0:T(8,128)(2,1)S(1)}, bf16[1,256,128]{2,1,0:T(8,128)(2,1)}, u32[]{:S(2)}) copy-start(bf16[1,256,128]{2,1,0:T(8,128)(2,1)} %param.9) | copy-start | bytes 196612
  7.2 110.0 %all-gather.3.cloned.1.call-start = ((), (), s32[]{:S(2)}) async-start(), calls=%async_computation.5 | async-start | bytes 4325376 | tf_op jit(solution)/shard_map/all_gather | solution.py:241
  9.6 12.1 %collective-permute-start = (bf16[2,256,128]{2,1,0:T(8,128)(2,1)S(1)}, bf16[2,256,128]{2,1,0:T(8,128)(2,1)S(1)}, u32[]{:S(2)}, u32[]{:S(2)}) collective-permute-start(bf16[2,256,128]{2,1,0:T(8,128)(2,1)S(1)} %pad_maximum_fusion), channel_id=1, source_target_pairs={{0,0},{1,8},{2,16},{3,24},{4,32},{5,40},{6,48},{7,56},{8,64},{9,72... | collective-permute-start | bytes 393224 | tf_op jit(solution)/shard_map/ppermute | solution.py:241
  21.7 0.7 copy-start.5
  22.4 5.3 %collective-permute-start.1 = (bf16[64,256]{1,0:T(8,128)(2,1)}, bf16[64,256]{1,0:T(8,128)(2,1)S(1)}, u32[]{:S(2)}, u32[]{:S(2)}) collective-permute-start(bf16[64,256]{1,0:T(8,128)(2,1)} %bitcast.48), channel_id=1, source_target_pairs={{0,16},{16,0},{1,17},{17,1},{2,18},{18,2},{3,19},{19,3},{4,20},{20... | collective-permute-start | bytes 98312 | tf_op jit(solution)/shard_map/ppermute | solution.py:245
  59.6 7.2 %collective-permute-start.2 = (bf16[8,2,64,256]{3,2,1,0:T(8,128)(2,1)S(1)}, bf16[8,2,64,256]{3,2,1,0:T(8,128)(2,1)S(1)}, u32[]{:S(2)}, u32[]{:S(2)}) collective-permute-start(bf16[8,2,64,256]{3,2,1,0:T(8,128)(2,1)S(1)} %all_to_all.25), channel_id=1, source_target_pairs={{0,1},{1,0},{2,3},{3,2},{4,5},{5,4},{6,7},{7,6},{8,9},{9,8},{10,11... | collective-permute-start | bytes 1572872 | tf_op jit(solution)/shard_map/ppermute | solution.py:249
  60.5 16.8 %all-to-all-start.1 = ((bf16[8,256,128]{2,1,0:T(8,128)(2,1)}), bf16[8,256,128]{2,1,0:T(8,128)(2,1)S(1)}, u32[]{:S(2)}, u32[]{:S(2)}) async-start(bf16[8,256,128]{2,1,0:T(8,128)(2,1)} %broadcast_in_dim.50), calls=%async_computation.1 | async-start | bytes 1048576 | tf_op jit(solution)/shard_map/all_to_all | solution.py:33
  68.1 28.0 %copy-start.4 = (bf16[1,256,128]{2,1,0:T(8,128)(2,1)S(1)}, bf16[1,256,128]{2,1,0:T(8,128)(2,1)}, u32[]{:S(2)}) copy-start(bf16[1,256,128]{2,1,0:T(8,128)(2,1)} %param.10) | copy-start | bytes 196612
  77.3 0.8 copy-start.2
  96.9 15.5 %all-to-all-start.4 = ((bf16[8,256,128]{2,1,0:T(8,128)(2,1)}), bf16[8,256,128]{2,1,0:T(8,128)(2,1)S(1)}, u32[]{:S(2)}, u32[]{:S(2)}) async-start(bf16[8,256,128]{2,1,0:T(8,128)(2,1)} %broadcast_in_dim.53), calls=%async_computation.4 | async-start | bytes 1048576 | tf_op jit(solution)/shard_map/all_to_all | solution.py:33
  112.5 9.2 %copy-start = (bf16[8,256,128]{2,1,0:T(8,128)(2,1)}, bf16[8,256,128]{2,1,0:T(8,128)(2,1)S(1)}, u32[]{:S(2)}) copy-start(bf16[8,256,128]{2,1,0:T(8,128)(2,1)S(1)} %all-to-all-done.4) | copy-start | bytes 1572868
  113.4 16.1 %all-to-all-start.3 = ((bf16[8,256,128]{2,1,0:T(8,128)(2,1)}), bf16[8,256,128]{2,1,0:T(8,128)(2,1)S(1)}, u32[]{:S(2)}, u32[]{:S(2)}) async-start(bf16[8,256,128]{2,1,0:T(8,128)(2,1)} %broadcast_in_dim.51), calls=%async_computation.3 | async-start | bytes 1048576 | tf_op jit(solution)/shard_map/all_to_all | solution.py:33
  129.5 0.8 copy-start.1
Sparse Core Ops, SparseCore 0:
  22.5 81.4 all-gather.2

commit v2 on v1

v2 whole, which is shorter than its diff:
```python
import jax
import jax.numpy as jnp
from jax import lax
from jax.experimental import pallas as pl
from jax.experimental.pallas import tpu as pltpu
from jax.sharding import Mesh
from jax.sharding import PartitionSpec as P


BF = jnp.bfloat16
F32 = jnp.float32
TILE = 2048
RANK = 128
GOAL = 64
STEP = 4
ROWS = 8
COLS = 32
OWN = 4
ROW = ("x", "yh")
COL = ("yl", "z", "core")
ALL = ("x", "yh", "yl", "z", "core")
SWAP = [(0, 1), (1, 0)]


ALONG_Z = [
    (z * 2 + core, (z + 1 - 2 * core) % 8 * 2 + core) for z in range(8) for core in range(2)
]


def to_tile_rows():
    pairs = []
    for x in range(4):
        for yh in range(2):
            for tile in range(COLS):
                row, k = divmod(tile, OWN)
                middle = row // 2 % 2 * 4 + row % 2 * 2
                z = (middle + 1 + x if k // 2 else middle - x) % 8
                pairs.append(((x * 2 + yh) * COLS + tile, row * COLS + yh * 16 + z * 2 + k % 2))
    return pairs


def held_rows(yl, z, core):
    middle = lax.rem(lax.axis_index("x"), 2) * 4 + lax.axis_index("yh") * 2
    ahead = lax.rem(z + 8 - middle, 8)
    above = (ahead >= 1) & (ahead <= 4)
    x = jnp.where(above, ahead - 1, lax.rem(8 - ahead, 8))
    return jnp.where(above, 2, 0) + core, pl.multiple_of((x * 2 + yl) * 256, 256)


def place(hop, swapped, other, flipped):
    yl, z, core = lax.axis_index("yl"), lax.axis_index("z"), lax.axis_index("core")
    way = 1 - 2 * core
    return (
        lax.rem(yl + flipped, 2),
        lax.rem(z + 8 + (way if other else -way) * hop, 8),
        lax.rem(core + (1 if other else 0) + swapped, 2),
    )


def dot_tn(a, b, precision=None):
    return lax.dot_general(
        a, b, (((0,), (0,)), ((), ())), precision=precision, preferred_element_type=F32
    )


def dot_nt(a, b, precision=None):
    return lax.dot_general(
        a, b, (((1,), (1,)), ((), ())), precision=precision, preferred_element_type=F32
    )


def dot_nn(a, b, precision=None):
    return lax.dot_general(
        a, b, (((1,), (0,)), ((), ())), precision=precision, preferred_element_type=F32
    )


def keep_kernel(rank_ref, left_ref, right_ref, own_ref, copies_ref):
    col = lax.broadcasted_iota(jnp.int32, (256, RANK), 1)
    kept = jnp.where(col < rank_ref[0], left_ref[0].astype(F32), 0.0).astype(BF)
    own_ref[0] = kept
    own_ref[1] = right_ref[0]
    for n in range(ROWS):
        copies_ref[n, 0] = kept
        copies_ref[n, 1] = right_ref[0]


def keep(rank, left, right):
    vmem = pl.BlockSpec(memory_space=pltpu.VMEM)
    return pl.pallas_call(
        keep_kernel,
        in_specs=[pl.BlockSpec(memory_space=pltpu.SMEM), vmem, vmem],
        out_shape=[
            jax.ShapeDtypeStruct((2, 256, RANK), BF),
            jax.ShapeDtypeStruct((ROWS, 2, 256, RANK), BF),
        ],
        compiler_params=pltpu.CompilerParams(vmem_limit_bytes=60 << 20),
        cost_estimate=pl.CostEstimate(
            flops=256 * RANK, bytes_accessed=1280 << 10, transcendentals=0
        ),
        name="keep",
    )(rank, left, right)


def solve_kernel(*refs):
    pieces, uy_ref, out_ref, lt = refs[:8], refs[8], refs[9], refs[10]
    for n, piece in enumerate(pieces):
        hop, other = (n, False) if n < 5 else (n - 4, True)
        for swapped in range(2):
            for flipped in range(2):
                yl, z, core = place(hop, swapped, other, flipped)
                start = pl.multiple_of((yl * 16 + z * 2 + core) * 64, 64)
                lt[pl.ds(start, 64), :] = piece[swapped, flipped]
    u_whole = uy_ref[:, 0].reshape(TILE, RANK)
    solved_t = dot_tn(u_whole, lt[...]).astype(BF)
    out_ref[...] = dot_nt(lt[...], solved_t).astype(BF).reshape(ROWS, 256, RANK)


def solve(l_pieces, uy):
    return pl.pallas_call(
        solve_kernel,
        out_shape=jax.ShapeDtypeStruct((ROWS, 256, RANK), BF),
        scratch_shapes=[pltpu.VMEM((TILE, 256), BF)],
        compiler_params=pltpu.CompilerParams(vmem_limit_bytes=10 << 20),
        cost_estimate=pl.CostEstimate(
            flops=4 * TILE * 256 * RANK, bytes_accessed=2 << 20, transcendentals=0
        ),
        name="solve",
    )(*l_pieces, uy)


def total_kernel(parts_ref, out_ref):
    total = parts_ref[0].astype(F32)
    for n in range(1, ROWS):
        total = total + parts_ref[n].astype(F32)
    out_ref[...] = total.astype(BF)


def total(parts):
    return pl.pallas_call(
        total_kernel,
        out_shape=jax.ShapeDtypeStruct((256, RANK), BF),
        compiler_params=pltpu.CompilerParams(vmem_limit_bytes=4 << 20),
        cost_estimate=pl.CostEstimate(
            flops=ROWS * 256 * RANK, bytes_accessed=576 << 10, transcendentals=0
        ),
        name="total",
    )(parts)


def probe_kernel(rank_ref, goal_ref, sketch_ref, uy_ref, right_ref, probe_ref, seen_ref):
    k = pl.program_id(0)
    row = lax.broadcasted_iota(jnp.int32, (RANK, RANK), 0)
    col = lax.broadcasted_iota(jnp.int32, (RANK, RANK), 1)
    core = dot_tn(right_ref[0], sketch_ref[...])
    keep = (row < rank_ref[k]) & (col < goal_ref[k])
    probe_ref[0] = jnp.where(keep, core, 0.0).astype(BF)

    @pl.when(k == 0)
    def _():
        seen_ref[...] = dot_tn(uy_ref[:, 1].reshape(TILE, RANK), sketch_ref[...])


def probe(ranks, goals, sketch, uy, right):
    return pl.pallas_call(
        probe_kernel,
        grid_spec=pltpu.PrefetchScalarGridSpec(
            num_scalar_prefetch=2,
            grid=(OWN,),
            in_specs=[
                pl.BlockSpec((TILE, RANK), lambda k, *_: (0, 0)),
                pl.BlockSpec((ROWS, 2, 256, RANK), lambda k, *_: (0, 0, 0, 0)),
                pl.BlockSpec((1, TILE, RANK), lambda k, *_: (k, 0, 0)),
            ],
            out_specs=[
                pl.BlockSpec((1, RANK, RANK), lambda k, *_: (k, 0, 0)),
                pl.BlockSpec((RANK, RANK), lambda k, *_: (0, 0)),
            ],
        ),
        out_shape=[
            jax.ShapeDtypeStruct((OWN, RANK, RANK), BF),
            jax.ShapeDtypeStruct((RANK, RANK), F32),
        ],
        compiler_params=pltpu.CompilerParams(vmem_limit_bytes=10 << 20),
        cost_estimate=pl.CostEstimate(
            flops=(OWN + 1) * 2 * TILE * RANK * RANK, bytes_accessed=4 << 20, transcendentals=0
        ),
        name="probe",
    )(ranks, goals, sketch, uy, right)


def before_kernel(left_hbm, *refs):
    pieces = refs[:16]
    gram_ref, turn_ref, y_ref, left, u_rows, sem, piece_sem = refs[16:]
    load_left = pltpu.make_async_copy(left_hbm, left, sem.at[0])
    load_left.start()
    moves = []
    for n, piece in enumerate(pieces):
        side, hop, other = (n % 2, n // 2, False) if n < 10 else (n % 2, (n - 8) // 2, True)
        for flipped in range(2):
            yl, z, core = place(hop, side, other, flipped)
            tile, start = held_rows(yl, z, core)
            for m, target in enumerate((u_rows, y_ref)):
                moves.append(
                    pltpu.make_async_copy(
                        piece.at[flipped, m],
                        target.at[tile, pl.ds(start, 256), :],
                        piece_sem.at[n, flipped, m],
                    )
                )
    for move in moves:
        move.start()
    for move in moves:
        move.wait()
    load_left.wait()

    @pl.loop(0, OWN)
    def _(k):
        turn_ref[k] = u_rows[k].T
        both = jnp.concatenate([left[k], y_ref[k]], axis=1)
        gram = dot_tn(both, both)
        first = gram.astype(BF)
        rest = gram - first.astype(F32)
        second = rest.astype(BF)
        gram_ref[k, 0:256, :] = first
        gram_ref[k, 256:512, :] = second
        gram_ref[k, 512:768, :] = (rest - second.astype(F32)).astype(BF)


def before(left, pieces):
    vmem = pl.BlockSpec(memory_space=pltpu.VMEM)
    hbm = pl.BlockSpec(memory_space=pl.ANY)
    return pl.pallas_call(
        before_kernel,
        in_specs=[hbm] * 17,
        out_specs=[vmem] * 3,
        out_shape=[
            jax.ShapeDtypeStruct((OWN, 768, 256), BF),
            jax.ShapeDtypeStruct((OWN, RANK, TILE), BF),
            jax.ShapeDtypeStruct((OWN, TILE, RANK), BF),
        ],
        scratch_shapes=[pltpu.VMEM((OWN, TILE, RANK), BF)] * 2
        + [pltpu.SemaphoreType.DMA((1,)), pltpu.SemaphoreType.DMA((16, 2, 2))],
        compiler_params=pltpu.CompilerParams(vmem_limit_bytes=18 << 20),
        cost_estimate=pl.CostEstimate(
            flops=OWN * 2 * TILE * 256 * 256, bytes_accessed=12 << 20, transcendentals=0
        ),
        name="before",
    )(left, *pieces)


def split(a, count):
    pieces = []
    for _ in range(count):
        pieces.append(a.astype(BF))
        a = a - pieces[-1].astype(F32)
    return pieces


def dot_fine(dot, a, b):
    a_high, a_low = split(a, 2)
    b_high, b_low = split(b, 2)
    return dot(a_high, b_high) + (dot(a_high, b_low) + dot(a_low, b_high))


def dot_exact(dot, a, b):
    high, middle, low = split(b, 3)
    return dot(a, high) + (dot(a, middle) + dot(a, low))


def whitening(grams):
    lane = lax.broadcasted_iota(jnp.int32, (8, RANK), 1)
    sub = lax.broadcasted_iota(jnp.int32, (8, RANK), 0)
    blocks = []
    for gram in grams:
        own = []
        for b in range(8):
            unit = jnp.where(lane == sub + (8 * b + GOAL), 1.0, 0.0)
            own.append(jnp.where(lane < GOAL, gram[8 * b : 8 * b + 8, :], unit))
        blocks.append(own)
    for first in range(0, GOAL, STEP):
        kb, top = first // 8, first % 8
        for own in blocks:
            columns = [
                [jnp.broadcast_to(own[b][:, first + j : first + j + 1], (8, RANK)) for j in range(STEP)]
                for b in range(kb, 8)
            ]
            rows = [
                jnp.broadcast_to(own[kb][top + i : top + i + 1, :], (8, RANK)) for i in range(STEP)
            ]
            corner = [
                [
                    jnp.broadcast_to(columns[0][j][top + i : top + i + 1, :], (8, RANK))
                    for j in range(STEP)
                ]
                for i in range(STEP)
            ]
            for j in range(STEP):
                inverse = 1.0 / corner[j][j]
                scaled = rows[j] * inverse
                ratio = [corner[j][m] * inverse for m in range(STEP)]
                for i in range(j + 1, STEP):
                    rows[i] = rows[i] - corner[i][j] * scaled
                    for m in range(j + 1, STEP):
                        corner[i][m] = corner[i][m] - corner[i][j] * ratio[m]
                for b in range(kb, 8):
                    column = columns[b - kb][j]
                    for m in range(j + 1, STEP):
                        columns[b - kb][m] = columns[b - kb][m] - column * ratio[m]
                    if b == kb:
                        column = jnp.where(sub > top + j, column, 0.0)
                    own[b] = own[b] - column * scaled
    factors = []
    for own in blocks:
        done = []
        for b in range(8):
            diagonal = jnp.sum(
                jnp.where(lane == sub + 8 * b, own[b], 0.0), axis=1, keepdims=True
            )
            scale = 1.0 / jnp.sqrt(diagonal)
            moved = pltpu.roll(own[b], GOAL, 1)
            done.append(jnp.where(lane < GOAL, moved * scale, 0.0))
        factors.append(jnp.concatenate(done, axis=0))
    return factors


def after_kernel(
    rank_ref, goal_ref, gram_ref, probe_ref, turn_ref, v0_ref, v1_ref, v2_ref, v3_ref,
    uy_ref, seen_ref, y_rows, left_hbm, right_hbm,
    out_left, out_right,
    left, right, v_ref, new_left, new_right, in_sem, out_sem,
):
    loads = []
    for n, (source, target) in enumerate(((left_hbm, left), (right_hbm, right))):
        copy = pltpu.make_async_copy(source, target, in_sem.at[n])
        copy.start()
        loads.append(copy)
    row = lax.broadcasted_iota(jnp.int32, (RANK, RANK), 0)
    col = lax.broadcasted_iota(jnp.int32, (RANK, RANK), 1)
    x, yh = lax.axis_index("x"), lax.axis_index("yh")
    for n, piece in enumerate((v0_ref, v1_ref, v2_ref, v3_ref)):
        for flipped in range(2):
            block = lax.rem(x + 4 - n, 4) * 2 + lax.rem(yh + flipped, 2)
            v_ref[pl.ds(pl.multiple_of(block * 256, 256), 256), :] = piece[flipped]
    y_whole = uy_ref[:, 1].reshape(TILE, RANK)
    right_probe = seen_ref[...]
    cores, probes, pushed, grams = [], [], [], []
    for k in range(OWN):
        core = dot_nn(turn_ref[k], v_ref[...])
        turned = dot_fine(dot_nn, core, jnp.where(col < goal_ref[k], right_probe, 0.0))
        probe = jnp.concatenate([probe_ref[k], (-turned).astype(BF)], axis=0)
        three = dot_nn(gram_ref[k], probe)
        push = three[0:256] + (three[256:512] + three[512:768])
        gram = dot_exact(dot_tn, probe, push) * (1.0 / TILE)
        gram = gram + jnp.where((row == col) & (col >= goal_ref[k]), 1.0, 0.0)
        cores.append(core)
        probes.append(probe)
        pushed.append(push)
        grams.append(gram[0:GOAL, :])
    factors = whitening(grams)
    zeros = jnp.zeros((RANK - GOAL, RANK), F32)
    mixes, backs, inners = [], [], []
    for k in range(OWN):
        factor = jnp.concatenate([factors[k], zeros], axis=0)
        mixed = dot_exact(dot_nt, probes[k], factor)
        high = mixed.astype(BF)
        mixes.append((high, (mixed - high.astype(F32)).astype(BF)))
        seen = dot_fine(dot_nt, pushed[k], factor)
        backs.append(jnp.where(row < rank_ref[k], seen[0:RANK], 0.0).astype(BF))
        inners.append(seen[RANK:])
    bents = [
        jnp.concatenate([backs[k], -dot_fine(dot_tn, cores[k], inners[k]).astype(BF)], axis=0)
        for k in range(OWN)
    ]
    for copy in loads:
        copy.wait()
    stores = []
    for k in range(OWN):
        high, low = mixes[k]
        both = jnp.concatenate([left[k], y_rows[k]], axis=1)
        new_left[k] = (dot_nn(both, high) + dot_nn(both, low)).astype(BF)
        copy = pltpu.make_async_copy(new_left.at[k], out_left.at[k], out_sem.at[0, k])
        copy.start()
        stores.append(copy)
        pair = jnp.concatenate([right[k], y_whole], axis=1)
        new_right[k] = (dot_nn(pair, bents[k]) * (1.0 / TILE)).astype(BF)
        copy = pltpu.make_async_copy(new_right.at[k], out_right.at[k], out_sem.at[1, k])
        copy.start()
        stores.append(copy)
    for copy in stores:
        copy.wait()


def after(ranks, goals, gram, probes, turn, v_pieces, uy, seen, y_rows, left, right):
    smem = pl.BlockSpec(memory_space=pltpu.SMEM)
    vmem = pl.BlockSpec(memory_space=pltpu.VMEM)
    hbm = pl.BlockSpec(memory_space=pl.ANY)
    whole = jax.ShapeDtypeStruct((OWN, TILE, RANK), BF)
    tiles = pltpu.VMEM((OWN, TILE, RANK), BF)
    return pl.pallas_call(
        after_kernel,
        in_specs=[smem, smem] + [vmem] * 10 + [hbm] * 2,
        out_specs=[hbm, hbm],
        out_shape=[whole, whole],
        scratch_shapes=[tiles, tiles, pltpu.VMEM((TILE, RANK), BF), tiles, tiles]
        + [pltpu.SemaphoreType.DMA((2,)), pltpu.SemaphoreType.DMA((2, OWN))],
        compiler_params=pltpu.CompilerParams(vmem_limit_bytes=24 << 20),
        cost_estimate=pl.CostEstimate(
            flops=OWN * 2 * TILE * 256 * RANK * 4, bytes_accessed=16 << 20, transcendentals=0
        ),
        name="after",
    )(ranks, goals, gram, probes, turn, *v_pieces, uy, seen, y_rows, left, right)


def swap(value, axis):
    return lax.ppermute(value, axis, SWAP)


def ring(value):
    return lax.ppermute(value, ("z", "core"), ALONG_Z)


def exchange(value):
    return lax.all_to_all(value, ROW, 0, 0, tiled=True)


def on_device(
    ba_left, ba_right, l_inverse, aa_left, aa_right, sketch, cross_tile_ranks, aa_rank, target_rank
):
    ranks, goals = aa_rank[:, 0], target_rank[:, 0]
    left, right = aa_left[:, 0], aa_right[:, 0]
    own, copies = keep(cross_tile_ranks, ba_left, ba_right)

    l_own = l_inverse.T
    l_pair = jnp.stack([l_own, swap(l_own, "yl")])
    l_chips = jnp.stack([l_pair, swap(l_pair, "core")])
    l_mine = [l_chips]
    for _ in range(1, 5):
        l_mine.append(ring(l_mine[-1]))
    l_pieces = l_mine + [swap(l_mine[hop], "core") for hop in range(1, 4)]
    uy = exchange(copies)

    moved = lax.ppermute(own, ALL, to_tile_rows())
    near = jnp.stack([moved, swap(moved, "yl")])
    mine = [(near, swap(near, "core"))]
    for _ in range(1, 5):
        mine.append((ring(mine[-1][0]), ring(mine[-1][1])))
    pieces = [half for pair in mine for half in pair]
    for hop in range(1, 4):
        pieces += [swap(mine[hop][0], "core"), swap(mine[hop][1], "core")]
    probes, seen = probe(ranks, goals, sketch, uy, right)
    gram, turn, y_rows = before(left, pieces)

    v_own = total(exchange(solve(l_pieces, uy)))
    v_pieces = [jnp.stack([v_own, swap(v_own, "yh")])]
    for hop in range(1, 4):
        v_pieces.append(
            lax.ppermute(v_pieces[0], "x", [(x, (x + hop) % 4) for x in range(4)])
        )
    new_left, new_right = after(
        ranks, goals, gram, probes, turn, v_pieces, uy, seen, y_rows, left, right
    )
    return new_left[:, None], new_right[:, None]


def solution(mesh):
    fine = Mesh(mesh.devices.reshape(4, 2, 2, 8, 2), ALL)
    in_specs = (
        P(COL, ROW, None),
        P(COL, ROW, None),
        P(ROW, COL),
        P(ROW, COL, None, None),
        P(ROW, COL, None, None),
        P(),
        P(COL),
        P(ROW, COL),
        P(ROW, COL),
    )
    out_specs = (P(ROW, COL, None, None), P(ROW, COL, None, None))
    return jax.shard_map(
        on_device, mesh=fine, in_specs=in_specs, out_specs=out_specs, check_vma=False
    )
```

time: 163 us -> 124 us (0.76)
  blocking collectives: 45.9 us -> 0 us
  starting transfers between devices: 29.4 us -> 63.6 us
  between operations: 14.8 us -> 1.69 us
  Pallas kernels: 35.3 us -> 26 us
  waiting for transfers between devices: 22.8 us -> 17.1 us
  local copies, waits for them, and re-layouts: 10.5 us -> 13.5 us
  other arithmetic: 2.74 us -> 0.07 us
    all_to_all x2 -> x0, blocking collectives: 45.9 us -> none  [the longest x1 31.1 us: gathered(): lax.all_to_all(jnp.broadcast_to(value[None], (count, *value.shape)), axis...]
    ppermute x3 -> x30, starting transfers between devices: 13.9 us -> 49.5 us  [the longest x14 28.5 us: swap(): return lax.ppermute(value, axis, SWAP)]
    all_to_all x3 -> x2, waiting for transfers between devices: 19.3 us -> 6.97 us  [exchange(): return lax.all_to_all(value, ROW, 0, 0, tiled=True)]
    unnamed x12 -> x48, local copies, waits for them, and re-layouts: 2.26 us -> 13.5 us
    pallas_call x3 -> x6, Pallas kernels: 35.3 us -> 26 us  [the longest x1 13.5 us: after(): pl.pallas_call(after_kernel, in_specs=[smem, smem] + [vmem] * 10 + [hbm]...]
    ppermute x3 -> x30, waiting for transfers between devices: 3.45 us -> 10.1 us  [the longest x12 6.51 us: ring(): return lax.ppermute(value, ('z', 'core'), ALONG_Z)]
    slice x1 -> x0, local copies, waits for them, and re-layouts: 4.54 us -> none  [per_device(): u_rows, y_rows = (bulk[0], bulk[1])]
    broadcast_in_dim x4 -> x0, local copies, waits for them, and re-layouts: 2.71 us -> none  [gathered(): jnp.broadcast_to(value[None], (count, *value.shape))]
  transfers between devices with their start and end apart: 7 -> 32, of which waited for: 4 -> 6; matrix products, arithmetic and copies ran while one was open for 6% -> 0% of each run, Pallas kernels for 7% -> 10%
where the time goes in v2:
time: 124 us; the launch traced here: 122 us
  starting transfers between devices  63.6 us (51%)
  Pallas kernels  26 us (21%)
  waiting for transfers between devices  17.1 us (14%)
  local copies, waits for them, and re-layouts  13.5 us (11%)
  between operations  1.69 us (1%)
    ppermute x14, starting transfers between devices, swap(): return lax.ppermute(value, axis, SWAP)  28.5 us
    ppermute x12, starting transfers between devices, ring(): return lax.ppermute(value, ('z', 'core'), ALONG_Z)  17.9 us
    all_to_all x2, starting transfers between devices, exchange(): return lax.all_to_all(value, ROW, 0, 0, tiled=True)  14.1 us
    pallas_call x1, Pallas kernels, after(): pl.pallas_call(after_kernel, in_specs=[smem, smem] + [vmem] * 10 + [hbm]...  13.5 us
    unnamed x48, local copies, waits for them, and re-layouts  13.5 us
    all_to_all x2, waiting for transfers between devices, exchange(): return lax.all_to_all(value, ROW, 0, 0, tiled=True)  6.97 us
    ppermute x12, waiting for transfers between devices, ring(): return lax.ppermute(value, ('z', 'core'), ALONG_Z)  6.51 us
    pallas_call x1, Pallas kernels, before(): pl.pallas_call(before_kernel, in_specs=[hbm] * 17, out_specs=[vmem] * 3,...  5.9 us
  transfers between devices with their start and end apart: 32, of which 6 were waited for; matrix products, arithmetic and copies ran while one was open for 0% of the time, Pallas kernels for 10%

profile of v2, /device:TPU:1, one launch (start us, length us, event | category | flops | bytes accessed | tf_op | source)
XLA Modules:
  0.0 121.9 jit_solution(15382327593694451271)
XLA Ops:
  0.6 2.2 %collective-permute-start.17 = (bf16[64,256]{1,0:T(8,128)(2,1)}, bf16[64,256]{1,0:T(8,128)(2,1)S(1)}, u32[]{:S(2)}, u32[]{:S(2)}) collective-permute-start(bf16[64,256]{1,0:T(8,128)(2,1)} %bitcast.34), channel_id=1, source_target_pairs={{0,16},{16,0},{1,17},{17,1},{2,18},{18,2},{3,19},{19,3},{4,20},{20... | collective-permute-start | bytes 98312 | tf_op jit(solution)/shard_map/ppermute | solution.py:416
  3.5 2.0 %keep.1 = (bf16[2,256,128]{2,1,0:T(8,128)(2,1)}, bf16[8,2,256,128]{3,2,1,0:T(8,128)(2,1)}) custom-call(s32[1]{0:T(128)S(6)} %copy.13.rank_ref, bf16[1,256,128]{2,1,0:T(8,128)(2,1)} %left_ref.1, bf16[1,256,128]{2,1,0:T(8,128)(2,1)} %right_ref.1), custom_call_target="tpu_custom_call" | custom-call | flops 32768 | bytes 1310720 | tf_op jit(solution)/shard_map/keep/pallas_call | solution.py:90
  5.5 6.5 %all-to-all-start = ((bf16[8,2,256,128]{3,2,1,0:T(8,128)(2,1)}), bf16[8,2,256,128]{3,2,1,0:T(8,128)(2,1)S(1)}, u32[]{:S(2)}, u32[]{:S(2)}) async-start(bf16[8,2,256,128]{3,2,1,0:T(8,128)(2,1)} %get-tuple-element.13), calls=%async_computation | async-start | bytes 2097152 | tf_op jit(solution)/shard_map/all_to_all | solution.py:424
  12.7 1.3 %collective-permute-start.18 = (bf16[2,64,256]{2,1,0:T(8,128)(2,1)S(1)}, bf16[2,64,256]{2,1,0:T(8,128)(2,1)S(1)}, u32[]{:S(2)}, u32[]{:S(2)}) collective-permute-start(bf16[2,64,256]{2,1,0:T(8,128)(2,1)S(1)} %get-tuple-element.23), channel_id=1, source_target_pairs={{0,1},{1,0},{2,3},{3,2},{4,5},{5,4},{6,7},{7,6},{8,9},{9,8},{10,11... | collective-permute-start | bytes 196616 | tf_op jit(solution)/shard_map/ppermute | solution.py:416
  14.1 16.1 %collective-permute-start.1 = (bf16[2,256,128]{2,1,0:T(8,128)(2,1)S(1)}, bf16[2,256,128]{2,1,0:T(8,128)(2,1)S(1)}, u32[]{:S(2)}, u32[]{:S(2)}) collective-permute-start(bf16[2,256,128]{2,1,0:T(8,128)(2,1)S(1)} %collective-permute-done), channel_id=1, source_target_pairs={{0,16},{16,0},{1,17},{17,1},{2,18},{18,2},{3,19},{19,3},{4,20},{20... | collective-permute-start | bytes 393224 | tf_op jit(solution)/shard_map/ppermute | solution.py:416
  30.2 3.2 %collective-permute-done.1 = bf16[2,256,128]{2,1,0:T(8,128)(2,1)S(1)} collective-permute-done((bf16[2,256,128]{2,1,0:T(8,128)(2,1)S(1)}, bf16[2,256,128]{2,1,0:T(8,128)(2,1)S(1)}, u32[]{:S(2)}, u32[]{:S(2)}) %collective-permute-start.1) | collective-permute-done | bytes 131104 | tf_op jit(solution)/shard_map/ppermute | solution.py:416
  33.4 1.3 %collective-permute-start.2 = (bf16[2,2,256,128]{3,2,1,0:T(8,128)(2,1)S(1)}, bf16[2,2,256,128]{3,2,1,0:T(8,128)(2,1)S(1)}, u32[]{:S(2)}, u32[]{:S(2)}) collective-permute-start(bf16[2,2,256,128]{3,2,1,0:T(8,128)(2,1)S(1)} %pad_maximum_fusion.refs_0_), channel_id=1, source_target_pairs={{0,1},{1,0},{2,3},{3,2},{4,5},{5,4},{6,7},{7,6},{8,9},{9,8},{10,11... | collective-permute-start | bytes 786440 | tf_op jit(solution)/shard_map/ppermute | solution.py:416
  34.7 3.2 %collective-permute-start.19 = (bf16[2,2,64,256]{3,2,1,0:T(8,128)(2,1)S(1)}, bf16[2,2,64,256]{3,2,1,0:T(8,128)(2,1)S(1)}, u32[]{:S(2)}, u32[]{:S(2)}) collective-permute-start(bf16[2,2,64,256]{3,2,1,0:T(8,128)(2,1)S(1)} %pad_maximum_fusion.1.refs_0_), channel_id=1, source_target_pairs={{0,2},{1,15},{2,4},{3,1},{4,6},{5,3},{6,8},{7,5},{8,10},{9,7},{10,... | collective-permute-start | bytes 393224 | tf_op jit(solution)/shard_map/ppermute | solution.py:420
  38.0 1.9 %collective-permute-done.19.refs_1_ = bf16[2,2,64,256]{3,2,1,0:T(8,128)(2,1)S(1)} collective-permute-done((bf16[2,2,64,256]{3,2,1,0:T(8,128)(2,1)S(1)}, bf16[2,2,64,256]{3,2,1,0:T(8,128)(2,1)S(1)}, u32[]{:S(2)}, u32[]{:S(2)}) %collective-permute-start.19) | collective-permute-done | bytes 131104 | tf_op jit(solution)/shard_map/ppermute | solution.py:420
  39.9 3.1 %collective-permute-start.20 = (bf16[2,2,64,256]{3,2,1,0:T(8,128)(2,1)S(1)}, bf16[2,2,64,256]{3,2,1,0:T(8,128)(2,1)S(1)}, u32[]{:S(2)}, u32[]{:S(2)}) collective-permute-start(bf16[2,2,64,256]{3,2,1,0:T(8,128)(2,1)S(1)} %collective-permute-done.19.refs_1_), channel_id=1, source_target_pairs={{0,2},{1,15},{2,4},{3,1},{4,6},{5,3},{6,8},{7,5},{8,10},{9,7},{10,... | collective-permute-start | bytes 393224 | tf_op jit(solution)/shard_map/ppermute | solution.py:420
  43.0 1.4 %collective-permute-start.3 = (bf16[2,2,256,128]{3,2,1,0:T(8,128)(2,1)S(1)}, bf16[2,2,256,128]{3,2,1,0:T(8,128)(2,1)}, u32[]{:S(2)}, u32[]{:S(2)}) collective-permute-start(bf16[2,2,256,128]{3,2,1,0:T(8,128)(2,1)S(1)} %pad_maximum_fusion.refs_0_), channel_id=1, source_target_pairs={{0,2},{1,15},{2,4},{3,1},{4,6},{5,3},{6,8},{7,5},{8,10},{9,7},{10,... | collective-permute-start | bytes 786440 | tf_op jit(solution)/shard_map/ppermute | solution.py:420
  45.1 2.9 %collective-permute-start.21 = (bf16[2,2,64,256]{3,2,1,0:T(8,128)(2,1)S(1)}, bf16[2,2,64,256]{3,2,1,0:T(8,128)(2,1)S(1)}, u32[]{:S(2)}, u32[]{:S(2)}) collective-permute-start(bf16[2,2,64,256]{3,2,1,0:T(8,128)(2,1)S(1)} %collective-permute-done.20.refs_2_), channel_id=1, source_target_pairs={{0,2},{1,15},{2,4},{3,1},{4,6},{5,3},{6,8},{7,5},{8,10},{9,7},{10,... | collective-permute-start | bytes 393224 | tf_op jit(solution)/shard_map/ppermute | solution.py:420
  49.8 2.9 %collective-permute-done.21.refs_3_ = bf16[2,2,64,256]{3,2,1,0:T(8,128)(2,1)S(1)} collective-permute-done((bf16[2,2,64,256]{3,2,1,0:T(8,128)(2,1)S(1)}, bf16[2,2,64,256]{3,2,1,0:T(8,128)(2,1)S(1)}, u32[]{:S(2)}, u32[]{:S(2)}) %collective-permute-start.21) | collective-permute-done | bytes 131104 | tf_op jit(solution)/shard_map/ppermute | solution.py:420
  52.8 1.7 %collective-permute-start.25 = (bf16[2,2,64,256]{3,2,1,0:T(8,128)(2,1)S(1)}, bf16[2,2,64,256]{3,2,1,0:T(8,128)(2,1)S(1)}, u32[]{:S(2)}, u32[]{:S(2)}) collective-permute-start(bf16[2,2,64,256]{3,2,1,0:T(8,128)(2,1)S(1)} %collective-permute-done.21.refs_3_), channel_id=1, source_target_pairs={{0,1},{1,0},{2,3},{3,2},{4,5},{5,4},{6,7},{7,6},{8,9},{9,8},{10,11... | collective-permute-start | bytes 393224 | tf_op jit(solution)/shard_map/ppermute | solution.py:416
  56.9 1.7 %collective-permute-start.5 = (bf16[2,2,256,128]{3,2,1,0:T(8,128)(2,1)}, bf16[2,2,256,128]{3,2,1,0:T(8,128)(2,1)}, u32[]{:S(2)}, u32[]{:S(2)}) collective-permute-start(bf16[2,2,256,128]{3,2,1,0:T(8,128)(2,1)} %collective-permute-done.3.refs_2_), channel_id=1, source_target_pairs={{0,2},{1,15},{2,4},{3,1},{4,6},{5,3},{6,8},{7,5},{8,10},{9,7},{10,... | collective-permute-start | bytes 786440 | tf_op jit(solution)/shard_map/ppermute | solution.py:420
  69.2 7.6 %all-to-all-start.1 = ((bf16[8,256,128]{2,1,0:T(8,128)(2,1)}), bf16[8,256,128]{2,1,0:T(8,128)(2,1)}, u32[]{:S(2)}, u32[]{:S(2)}) async-start(bf16[8,256,128]{2,1,0:T(8,128)(2,1)} %copy-done.2), calls=%async_computation.1 | async-start | bytes 1048576 | tf_op jit(solution)/shard_map/all_to_all | solution.py:424
  78.1 1.4 %collective-permute-start.13 = (bf16[2,2,256,128]{3,2,1,0:T(8,128)(2,1)}, bf16[2,2,256,128]{3,2,1,0:T(8,128)(2,1)}, u32[]{:S(2)}, u32[]{:S(2)}) collective-permute-start(bf16[2,2,256,128]{3,2,1,0:T(8,128)(2,1)} %collective-permute-done.5.refs_4_), channel_id=1, source_target_pairs={{0,1},{1,0},{2,3},{3,2},{4,5},{5,4},{6,7},{7,6},{8,9},{9,8},{10,11... | collective-permute-start | bytes 786440 | tf_op jit(solution)/shard_map/ppermute | solution.py:416
  80.7 7.0 %all-to-all-done.1.parts_ref = bf16[8,256,128]{2,1,0:T(8,128)(2,1)} async-done(((bf16[8,256,128]{2,1,0:T(8,128)(2,1)}), bf16[8,256,128]{2,1,0:T(8,128)(2,1)}, u32[]{:S(2)}, u32[]{:S(2)}) %all-to-all-start.1) | async-done | bytes 524320 | tf_op jit(solution)/shard_map/all_to_all | solution.py:424
  89.8 1.8 %collective-permute-start.15 = (bf16[2,2,256,128]{3,2,1,0:T(8,128)(2,1)}, bf16[2,2,256,128]{3,2,1,0:T(8,128)(2,1)S(1)}, u32[]{:S(2)}, u32[]{:S(2)}) collective-permute-start(bf16[2,2,256,128]{3,2,1,0:T(8,128)(2,1)} %collective-permute-done.7.refs_6_), channel_id=1, source_target_pairs={{0,1},{1,0},{2,3},{3,2},{4,5},{5,4},{6,7},{7,6},{8,9},{9,8},{10,11... | collective-permute-start | bytes 786440 | tf_op jit(solution)/shard_map/ppermute | solution.py:416
  95.7 1.6 %collective-permute-done.9.refs_8_ = bf16[2,2,256,128]{3,2,1,0:T(8,128)(2,1)S(1)} collective-permute-done((bf16[2,2,256,128]{3,2,1,0:T(8,128)(2,1)}, bf16[2,2,256,128]{3,2,1,0:T(8,128)(2,1)S(1)}, u32[]{:S(2)}, u32[]{:S(2)}) %collective-permute-start.9) | collective-permute-done | bytes 262176 | tf_op jit(solution)/shard_map/ppermute | solution.py:420
  97.6 1.2 collective-permute-start.27
  99.8 2.3 %probe.1 = (bf16[4,128,128]{2,1,0:T(8,128)(2,1)S(1)}, f32[128,128]{1,0:T(8,128)S(1)}) custom-call(s32[4]{0:T(128)S(1)} %bitcast.26, s32[4]{0:T(128)S(1)} %bitcast.28, bf16[2048,128]{1,0:T(8,128)(2,1)S(1)} %copy-done.3, bf16[8,2,256,128]{3,2,1,0:T(8,128)(2,1)S(1)} %all-to-all-done.uy_ref.refs_8_, bf16[4,2048,128]{2,1,0:T(8,128)(2,1)S(1)} %bitcast.23), custom_call_target="tpu_custom_call" | custom-call | flops 335544320 | bytes 4194304 | tf_op jit(solution)/shard_map/probe/pallas_call | solution.py:165
  102.2 5.9 %before.1 = (bf16[4,768,256]{2,1,0:T(8,128)(2,1)S(1)}, bf16[4,128,2048]{2,1,0:T(8,128)(2,1)S(1)}, bf16[4,2048,128]{2,1,0:T(8,128)(2,1)S(1)}) custom-call(bf16[4,2048,128]{2,1,0:T(8,128)(2,1)S(1)} %bitcast.21, bf16[2,2,256,128]{3,2,1,0:T(8,128)(2,1)S(1)} %pad_maximum_fusion.refs_0_, bf16[2,2,256,128]{3,2,1,0:T(8,128)(2,1)S(1)} %copy-done.5, ...), custom_call_target="tpu_custom_call" | custom-call | flops 1073741824 | bytes 12582912 | tf_op jit(solution)/shard_map/before/pallas_call | solution.py:233
  108.2 13.5 %after.1 = (bf16[4,2048,128]{2,1,0:T(8,128)(2,1)}, bf16[4,2048,128]{2,1,0:T(8,128)(2,1)}) custom-call(s32[4]{0:T(128)S(1)} %bitcast.27, s32[4]{0:T(128)S(1)} %bitcast.29, bf16[4,768,256]{2,1,0:T(8,128)(2,1)S(1)} %get-tuple-element.12.gram_ref, bf16[4,128,128]{2,1,0:T(8,128)(2,1)S(1)} %get-tuple-element.14.probe_ref, ...), custom_call_target="tpu_custom_call" | custom-call | flops 2147483648 | bytes 16777216 | tf_op jit(solution)/shard_map/after/pallas_call | solution.py:400
  (98 shorter events, 26.3 us)
Async XLA Ops:
  0.6 12.1 %collective-permute-start.17 = (bf16[64,256]{1,0:T(8,128)(2,1)}, bf16[64,256]{1,0:T(8,128)(2,1)S(1)}, u32[]{:S(2)}, u32[]{:S(2)}) collective-permute-start(bf16[64,256]{1,0:T(8,128)(2,1)} %bitcast.34), channel_id=1, source_target_pairs={{0,16},{16,0},{1,17},{17,1},{2,18},{18,2},{3,19},{19,3},{4,20},{20... | collective-permute-start | bytes 98312 | tf_op jit(solution)/shard_map/ppermute | solution.py:416
  5.5 55.5 %all-to-all-start = ((bf16[8,2,256,128]{3,2,1,0:T(8,128)(2,1)}), bf16[8,2,256,128]{3,2,1,0:T(8,128)(2,1)S(1)}, u32[]{:S(2)}, u32[]{:S(2)}) async-start(bf16[8,2,256,128]{3,2,1,0:T(8,128)(2,1)} %get-tuple-element.13), calls=%async_computation | async-start | bytes 2097152 | tf_op jit(solution)/shard_map/all_to_all | solution.py:424
  12.7 17.4 %collective-permute-start.18 = (bf16[2,64,256]{2,1,0:T(8,128)(2,1)S(1)}, bf16[2,64,256]{2,1,0:T(8,128)(2,1)S(1)}, u32[]{:S(2)}, u32[]{:S(2)}) collective-permute-start(bf16[2,64,256]{2,1,0:T(8,128)(2,1)S(1)} %get-tuple-element.23), channel_id=1, source_target_pairs={{0,1},{1,0},{2,3},{3,2},{4,5},{5,4},{6,7},{7,6},{8,9},{9,8},{10,11... | collective-permute-start | bytes 196616 | tf_op jit(solution)/shard_map/ppermute | solution.py:416
  14.1 19.3 %collective-permute-start.1 = (bf16[2,256,128]{2,1,0:T(8,128)(2,1)S(1)}, bf16[2,256,128]{2,1,0:T(8,128)(2,1)S(1)}, u32[]{:S(2)}, u32[]{:S(2)}) collective-permute-start(bf16[2,256,128]{2,1,0:T(8,128)(2,1)S(1)} %collective-permute-done), channel_id=1, source_target_pairs={{0,16},{16,0},{1,17},{17,1},{2,18},{18,2},{3,19},{19,3},{4,20},{20... | collective-permute-start | bytes 393224 | tf_op jit(solution)/shard_map/ppermute | solution.py:416
  33.4 11.0 %collective-permute-start.2 = (bf16[2,2,256,128]{3,2,1,0:T(8,128)(2,1)S(1)}, bf16[2,2,256,128]{3,2,1,0:T(8,128)(2,1)S(1)}, u32[]{:S(2)}, u32[]{:S(2)}) collective-permute-start(bf16[2,2,256,128]{3,2,1,0:T(8,128)(2,1)S(1)} %pad_maximum_fusion.refs_0_), channel_id=1, source_target_pairs={{0,1},{1,0},{2,3},{3,2},{4,5},{5,4},{6,7},{7,6},{8,9},{9,8},{10,11... | collective-permute-start | bytes 786440 | tf_op jit(solution)/shard_map/ppermute | solution.py:416
  43.0 13.9 %collective-permute-start.3 = (bf16[2,2,256,128]{3,2,1,0:T(8,128)(2,1)S(1)}, bf16[2,2,256,128]{3,2,1,0:T(8,128)(2,1)}, u32[]{:S(2)}, u32[]{:S(2)}) collective-permute-start(bf16[2,2,256,128]{3,2,1,0:T(8,128)(2,1)S(1)} %pad_maximum_fusion.refs_0_), channel_id=1, source_target_pairs={{0,2},{1,15},{2,4},{3,1},{4,6},{5,3},{6,8},{7,5},{8,10},{9,7},{10,... | collective-permute-start | bytes 786440 | tf_op jit(solution)/shard_map/ppermute | solution.py:420
  44.4 14.3 %collective-permute-start.4 = (bf16[2,2,256,128]{3,2,1,0:T(8,128)(2,1)S(1)}, bf16[2,2,256,128]{3,2,1,0:T(8,128)(2,1)}, u32[]{:S(2)}, u32[]{:S(2)}) collective-permute-start(bf16[2,2,256,128]{3,2,1,0:T(8,128)(2,1)S(1)} %collective-permute-done.2.refs_1_), channel_id=1, source_target_pairs={{0,2},{1,15},{2,4},{3,1},{4,6},{5,3},{6,8},{7,5},{8,10},{9,7},{10,... | collective-permute-start | bytes 786440 | tf_op jit(solution)/shard_map/ppermute | solution.py:420
  45.1 7.6 %collective-permute-start.21 = (bf16[2,2,64,256]{3,2,1,0:T(8,128)(2,1)S(1)}, bf16[2,2,64,256]{3,2,1,0:T(8,128)(2,1)S(1)}, u32[]{:S(2)}, u32[]{:S(2)}) collective-permute-start(bf16[2,2,64,256]{3,2,1,0:T(8,128)(2,1)S(1)} %collective-permute-done.20.refs_2_), channel_id=1, source_target_pairs={{0,2},{1,15},{2,4},{3,1},{4,6},{5,3},{6,8},{7,5},{8,10},{9,7},{10,... | collective-permute-start | bytes 393224 | tf_op jit(solution)/shard_map/ppermute | solution.py:420
  48.0 6.5 %collective-permute-start.23 = (bf16[2,2,64,256]{3,2,1,0:T(8,128)(2,1)S(1)}, bf16[2,2,64,256]{3,2,1,0:T(8,128)(2,1)S(1)}, u32[]{:S(2)}, u32[]{:S(2)}) collective-permute-start(bf16[2,2,64,256]{3,2,1,0:T(8,128)(2,1)S(1)} %collective-permute-done.19.refs_1_), channel_id=1, source_target_pairs={{0,1},{1,0},{2,3},{3,2},{4,5},{5,4},{6,7},{7,6},{8,9},{9,8},{10,11... | collective-permute-start | bytes 393224 | tf_op jit(solution)/shard_map/ppermute | solution.py:416
  48.9 10.1 %collective-permute-start.24 = (bf16[2,2,64,256]{3,2,1,0:T(8,128)(2,1)S(1)}, bf16[2,2,64,256]{3,2,1,0:T(8,128)(2,1)S(1)}, u32[]{:S(2)}, u32[]{:S(2)}) collective-permute-start(bf16[2,2,64,256]{3,2,1,0:T(8,128)(2,1)S(1)} %collective-permute-done.20.refs_2_), channel_id=1, source_target_pairs={{0,1},{1,0},{2,3},{3,2},{4,5},{5,4},{6,7},{7,6},{8,9},{9,8},{10,11... | collective-permute-start | bytes 393224 | tf_op jit(solution)/shard_map/ppermute | solution.py:416
  52.8 6.9 %collective-permute-start.25 = (bf16[2,2,64,256]{3,2,1,0:T(8,128)(2,1)S(1)}, bf16[2,2,64,256]{3,2,1,0:T(8,128)(2,1)S(1)}, u32[]{:S(2)}, u32[]{:S(2)}) collective-permute-start(bf16[2,2,64,256]{3,2,1,0:T(8,128)(2,1)S(1)} %collective-permute-done.21.refs_3_), channel_id=1, source_target_pairs={{0,1},{1,0},{2,3},{3,2},{4,5},{5,4},{6,7},{7,6},{8,9},{9,8},{10,11... | collective-permute-start | bytes 393224 | tf_op jit(solution)/shard_map/ppermute | solution.py:416
  56.9 20.5 %collective-permute-start.5 = (bf16[2,2,256,128]{3,2,1,0:T(8,128)(2,1)}, bf16[2,2,256,128]{3,2,1,0:T(8,128)(2,1)}, u32[]{:S(2)}, u32[]{:S(2)}) collective-permute-start(bf16[2,2,256,128]{3,2,1,0:T(8,128)(2,1)} %collective-permute-done.3.refs_2_), channel_id=1, source_target_pairs={{0,2},{1,15},{2,4},{3,1},{4,6},{5,3},{6,8},{7,5},{8,10},{9,7},{10,... | collective-permute-start | bytes 786440 | tf_op jit(solution)/shard_map/ppermute | solution.py:420
  58.7 20.9 %collective-permute-start.6 = (bf16[2,2,256,128]{3,2,1,0:T(8,128)(2,1)}, bf16[2,2,256,128]{3,2,1,0:T(8,128)(2,1)}, u32[]{:S(2)}, u32[]{:S(2)}) collective-permute-start(bf16[2,2,256,128]{3,2,1,0:T(8,128)(2,1)} %collective-permute-done.4.refs_3_), channel_id=1, source_target_pairs={{0,2},{1,15},{2,4},{3,1},{4,6},{5,3},{6,8},{7,5},{8,10},{9,7},{10,... | collective-permute-start | bytes 786440 | tf_op jit(solution)/shard_map/ppermute | solution.py:420
  69.2 18.5 %all-to-all-start.1 = ((bf16[8,256,128]{2,1,0:T(8,128)(2,1)}), bf16[8,256,128]{2,1,0:T(8,128)(2,1)}, u32[]{:S(2)}, u32[]{:S(2)}) async-start(bf16[8,256,128]{2,1,0:T(8,128)(2,1)} %copy-done.2), calls=%async_computation.1 | async-start | bytes 1048576 | tf_op jit(solution)/shard_map/all_to_all | solution.py:424
  76.8 12.0 %collective-permute-start.11 = (bf16[2,2,256,128]{3,2,1,0:T(8,128)(2,1)}, bf16[2,2,256,128]{3,2,1,0:T(8,128)(2,1)}, u32[]{:S(2)}, u32[]{:S(2)}) collective-permute-start(bf16[2,2,256,128]{3,2,1,0:T(8,128)(2,1)} %collective-permute-done.3.refs_2_), channel_id=1, source_target_pairs={{0,1},{1,0},{2,3},{3,2},{4,5},{5,4},{6,7},{7,6},{8,9},{9,8},{10,11... | collective-permute-start | bytes 786440 | tf_op jit(solution)/shard_map/ppermute | solution.py:416
  77.4 12.4 %collective-permute-start.7 = (bf16[2,2,256,128]{3,2,1,0:T(8,128)(2,1)}, bf16[2,2,256,128]{3,2,1,0:T(8,128)(2,1)}, u32[]{:S(2)}, u32[]{:S(2)}) collective-permute-start(bf16[2,2,256,128]{3,2,1,0:T(8,128)(2,1)} %collective-permute-done.5.refs_4_), channel_id=1, source_target_pairs={{0,2},{1,15},{2,4},{3,1},{4,6},{5,3},{6,8},{7,5},{8,10},{9,7},{10,... | collective-permute-start | bytes 786440 | tf_op jit(solution)/shard_map/ppermute | solution.py:420
  78.1 13.4 %collective-permute-start.13 = (bf16[2,2,256,128]{3,2,1,0:T(8,128)(2,1)}, bf16[2,2,256,128]{3,2,1,0:T(8,128)(2,1)}, u32[]{:S(2)}, u32[]{:S(2)}) collective-permute-start(bf16[2,2,256,128]{3,2,1,0:T(8,128)(2,1)} %collective-permute-done.5.refs_4_), channel_id=1, source_target_pairs={{0,1},{1,0},{2,3},{3,2},{4,5},{5,4},{6,7},{7,6},{8,9},{9,8},{10,11... | collective-permute-start | bytes 786440 | tf_op jit(solution)/shard_map/ppermute | solution.py:416
  79.6 13.1 %collective-permute-start.12 = (bf16[2,2,256,128]{3,2,1,0:T(8,128)(2,1)}, bf16[2,2,256,128]{3,2,1,0:T(8,128)(2,1)}, u32[]{:S(2)}, u32[]{:S(2)}) collective-permute-start(bf16[2,2,256,128]{3,2,1,0:T(8,128)(2,1)} %collective-permute-done.4.refs_3_), channel_id=1, source_target_pairs={{0,1},{1,0},{2,3},{3,2},{4,5},{5,4},{6,7},{7,6},{8,9},{9,8},{10,11... | collective-permute-start | bytes 786440 | tf_op jit(solution)/shard_map/ppermute | solution.py:416
  79.6 13.5 %collective-permute-start.8 = (bf16[2,2,256,128]{3,2,1,0:T(8,128)(2,1)}, bf16[2,2,256,128]{3,2,1,0:T(8,128)(2,1)}, u32[]{:S(2)}, u32[]{:S(2)}) collective-permute-start(bf16[2,2,256,128]{3,2,1,0:T(8,128)(2,1)} %collective-permute-done.6.refs_5_), channel_id=1, source_target_pairs={{0,2},{1,15},{2,4},{3,1},{4,6},{5,3},{6,8},{7,5},{8,10},{9,7},{10,... | collective-permute-start | bytes 786440 | tf_op jit(solution)/shard_map/ppermute | solution.py:420
  93.1 9.1 %collective-permute-start.16 = (bf16[2,2,256,128]{3,2,1,0:T(8,128)(2,1)}, bf16[2,2,256,128]{3,2,1,0:T(8,128)(2,1)S(1)}, u32[]{:S(2)}, u32[]{:S(2)}) collective-permute-start(bf16[2,2,256,128]{3,2,1,0:T(8,128)(2,1)} %collective-permute-done.8.refs_7_), channel_id=1, source_target_pairs={{0,1},{1,0},{2,3},{3,2},{4,5},{5,4},{6,7},{7,6},{8,9},{9,8},{10,11... | collective-permute-start | bytes 786440 | tf_op jit(solution)/shard_map/ppermute | solution.py:416
  93.5 8.6 %collective-permute-start.10 = (bf16[2,2,256,128]{3,2,1,0:T(8,128)(2,1)}, bf16[2,2,256,128]{3,2,1,0:T(8,128)(2,1)S(1)}, u32[]{:S(2)}, u32[]{:S(2)}) collective-permute-start(bf16[2,2,256,128]{3,2,1,0:T(8,128)(2,1)} %collective-permute-done.8.refs_7_), channel_id=1, source_target_pairs={{0,2},{1,15},{2,4},{3,1},{4,6},{5,3},{6,8},{7,5},{8,10},{9,7},{10,... | collective-permute-start | bytes 786440 | tf_op jit(solution)/shard_map/ppermute | solution.py:420
  94.8 13.4 %collective-permute-start.29 = (bf16[2,256,128]{2,1,0:T(8,128)(2,1)S(1)}, bf16[2,256,128]{2,1,0:T(8,128)(2,1)S(1)}, u32[]{:S(2)}, u32[]{:S(2)}) collective-permute-start(bf16[2,256,128]{2,1,0:T(8,128)(2,1)S(1)} %pad_maximum_fusion.2.v0_ref), channel_id=1, source_target_pairs={{0,192},{64,0},{128,64},{192,128},{1,193},{65,1},{129,65},{193,129... | collective-permute-start | bytes 393224 | tf_op jit(solution)/shard_map/ppermute | solution.py:458
  97.3 10.8 %collective-permute-start.28 = (bf16[2,256,128]{2,1,0:T(8,128)(2,1)S(1)}, bf16[2,256,128]{2,1,0:T(8,128)(2,1)S(1)}, u32[]{:S(2)}, u32[]{:S(2)}) collective-permute-start(bf16[2,256,128]{2,1,0:T(8,128)(2,1)S(1)} %pad_maximum_fusion.2.v0_ref), channel_id=1, source_target_pairs={{0,128},{64,192},{128,0},{192,64},{1,129},{65,193},{129,1},{193,65... | collective-permute-start | bytes 393224 | tf_op jit(solution)/shard_map/ppermute | solution.py:458
  97.6 10.5 %collective-permute-start.27 = (bf16[2,256,128]{2,1,0:T(8,128)(2,1)S(1)}, bf16[2,256,128]{2,1,0:T(8,128)(2,1)S(1)}, u32[]{:S(2)}, u32[]{:S(2)}) collective-permute-start(bf16[2,256,128]{2,1,0:T(8,128)(2,1)S(1)} %pad_maximum_fusion.2.v0_ref), channel_id=1, source_target_pairs={{0,64},{64,128},{128,192},{192,0},{1,65},{65,129},{129,193},{193,1... | collective-permute-start | bytes 393224 | tf_op jit(solution)/shard_map/ppermute | solution.py:458
  (32 other events, 294.2 us)
